TPU v7x, 32 devices: a whole 2x2x4 slice. The times are simulated.
32 devices in a mesh: dp: 4 (over z), blk: 2 (over y), head: 4 (over x, core).
Axes of the slice: x: 2, y: 2, z: 4, core: 2. Of those that a mesh axis runs over, the one named last changes fastest.
Arguments:
- tokens: bfloat16 [4, 2048, 768], P('dp', ('blk', 'head')), may hold values from -6 to 6
- cond: bfloat16 [4, 128], P('dp'), may hold values from -6 to 6
- lengths: int32 [4], P('dp'), may hold values from 1024 to 2048, as said below
- ada_weight: bfloat16 [128, 4608], P(None, ('dp', 'blk', 'head')), may hold values from -0.5 to 0.5
- ada_bias: bfloat16 [4608], P(('dp', 'blk', 'head')), may hold values from -4 to 4
- norm1_gain: bfloat16 [768], P(('dp', 'blk', 'head')), may hold values from 0.5 to 1.5
- qkv_weight: bfloat16 [768, 2304], P(None, ('dp', 'blk', 'head')), may hold values from -0.15136719 to 0.15136719
- out_weight: bfloat16 [768, 768], P(None, ('dp', 'blk', 'head')), may hold values from -3.078125 to 3.078125
- norm2_gain: bfloat16 [768], P(('dp', 'blk', 'head')), may hold values from 0.5 to 1.5
- up_weight: bfloat16 [768, 3072], P(None, ('dp', 'blk', 'head')), may hold values from -0.21875 to 0.21875
- up_bias: bfloat16 [3072], P(('dp', 'blk', 'head')), may hold values from -4 to 4
- down_weight: bfloat16 [3072, 768], P(None, ('dp', 'blk', 'head')), may hold values from -0.109375 to 0.109375
- down_bias: bfloat16 [768], P(('dp', 'blk', 'head')), may hold values from -4 to 4
- out_grad: bfloat16 [4, 2048, 768], P('dp', ('blk', 'head')), may hold values from -6 to 6
Outputs:
- mixed: bfloat16 [4, 2048, 768], P('dp', ('blk', 'head'))
- tokens_grad: float32 [4, 2048, 768], P('dp', ('blk', 'head'))
- cond_grad: float32 [4, 128], P('dp')
- ada_weight_grad: float32 [128, 4608], P(None, ('dp', 'blk', 'head'))
- ada_bias_grad: float32 [4608], P(('dp', 'blk', 'head'))
- norm1_gain_grad: float32 [768], P(('dp', 'blk', 'head'))
- qkv_weight_grad: float32 [768, 2304], P(None, ('dp', 'blk', 'head'))
- out_weight_grad: float32 [768, 768], P(None, ('dp', 'blk', 'head'))
- norm2_gain_grad: float32 [768], P(('dp', 'blk', 'head'))
- up_weight_grad: float32 [768, 3072], P(None, ('dp', 'blk', 'head'))
- up_bias_grad: float32 [3072], P(('dp', 'blk', 'head'))
- down_weight_grad: float32 [3072, 768], P(None, ('dp', 'blk', 'head'))
- down_bias_grad: float32 [768], P(('dp', 'blk', 'head'))
Inputs may be any that keep to these rules, and one draw needn't show every extreme that they name: Row r holds one sequence in its slots 0 to lengths[r] - 1, the rest is padding; some row is full and some row is half full.
All inputs are finite; a program needn't handle non-finite values.
Results may differ from a plain program's by a relative error of at most 0.034.
Values may be sent and summed in bfloat16 or wider, within the bound.
A program may use at most 128 MiB of HBM per device.

v0:
```python
from functools import partial
import math

import jax
import jax.numpy as jnp
from jax import lax
from jax.sharding import PartitionSpec as P

HEADS = 12
HEAD_DIM = 64


EPSILON = 1e-05
NEG_LARGE = -1e30
HIGHEST = lax.Precision.HIGHEST


def rotary_tables(positions):
    half_dim = HEAD_DIM // 2
    frequency = jnp.exp(
        jnp.arange(half_dim, dtype=jnp.float32) * (-2.0 * math.log(10000.0) / HEAD_DIM)
    )
    angles = positions.astype(jnp.float32)[:, None] * frequency[None, :]
    return (jnp.cos(angles), jnp.sin(angles))


def rotate(values, cosine, sine):
    half_dim = HEAD_DIM // 2
    first_half = values[..., :half_dim]
    second_half = values[..., half_dim:]
    cos_wide = cosine[:, None, :]
    sin_wide = sine[:, None, :]
    return jnp.concatenate(
        [
            first_half * cos_wide - second_half * sin_wide,
            second_half * cos_wide + first_half * sin_wide,
        ],
        axis=-1,
    )


def rotate_back(grads, cosine, sine):
    half_dim = HEAD_DIM // 2
    first_half = grads[..., :half_dim]
    second_half = grads[..., half_dim:]
    cos_wide = cosine[:, None, :]
    sin_wide = sine[:, None, :]
    return jnp.concatenate(
        [
            first_half * cos_wide + second_half * sin_wide,
            second_half * cos_wide - first_half * sin_wide,
        ],
        axis=-1,
    )


def normalize(values):
    center = values - jnp.mean(values, axis=-1, keepdims=True)
    inverse = lax.rsqrt(jnp.mean(center * center, axis=-1, keepdims=True) + EPSILON)
    return (center * inverse, inverse)


def normalize_back(grad_unit, unit_values, inverse):
    mean_grad = jnp.mean(grad_unit, axis=-1, keepdims=True)
    mean_cross = jnp.mean(grad_unit * unit_values, axis=-1, keepdims=True)
    return (grad_unit - mean_grad - unit_values * mean_cross) * inverse


def block_size(count_rows):
    return math.gcd(count_rows, 1024)


def key_window(piece_array, offset, step_rows, heads_local):
    window = lax.dynamic_slice_in_dim(piece_array, offset, step_rows, 1)
    return window.reshape(window.shape[0], step_rows, heads_local, HEAD_DIM)


def score_grads(
    query_block, grad_block, key_block, value_block, log_block, delta_block, key_live, score_scale
):
    scores = (
        jnp.einsum("rqhd,rkhd->rhqk", query_block, key_block, preferred_element_type=jnp.float32)
        * score_scale
    )
    probs = jnp.where(key_live, jnp.exp(scores - log_block[..., None]), 0.0)
    grad_probs = jnp.einsum(
        "rqhd,rkhd->rhqk", grad_block, value_block, preferred_element_type=jnp.float32
    )
    grad_scores = (probs * (grad_probs - delta_block[..., None])).astype(jnp.bfloat16)
    return (probs.astype(jnp.bfloat16), grad_scores)


def attend_fold(queries, lengths, score_scale, running, piece_rows):
    heads_local = queries.shape[2]
    key_piece, value_piece = piece_rows
    piece_len = key_piece.shape[1]
    step_rows = block_size(piece_len)

    def attend_one_step(step_index, loop_state):
        row_peak, row_total, summed = loop_state
        offset = step_index * step_rows
        key_block = key_window(key_piece, offset, step_rows, heads_local)
        value_block = key_window(value_piece, offset, step_rows, heads_local)
        positions = offset + jnp.arange(step_rows, dtype=jnp.int32)
        key_live = (positions[None, :] < lengths[:, None])[:, None, None, :]
        scores = (
            jnp.einsum("rqhd,rkhd->rhqk", queries, key_block, preferred_element_type=jnp.float32)
            * score_scale
        )
        scores = jnp.where(key_live, scores, NEG_LARGE)
        new_peak = jnp.maximum(row_peak, jnp.max(scores, axis=-1))
        weights = jnp.where(key_live, jnp.exp(scores - new_peak[..., None]), 0.0)
        fade_factor = jnp.exp(row_peak - new_peak)
        row_total = row_total * fade_factor + jnp.sum(weights, axis=-1)
        update = jnp.einsum(
            "rhqk,rkhd->rqhd",
            weights.astype(jnp.bfloat16),
            value_block,
            preferred_element_type=jnp.float32,
        )
        summed = summed * jnp.transpose(fade_factor, (0, 2, 1))[..., None] + update
        return (new_peak, row_total, summed)

    return lax.fori_loop(0, piece_len // step_rows, attend_one_step, running)


def query_fold(
    queries, grad_heads, log_total, row_delta, lengths, score_scale, running, piece_rows
):
    heads_local = queries.shape[2]
    key_piece, value_piece = piece_rows
    piece_len = key_piece.shape[1]
    step_rows = block_size(piece_len)

    def query_one_step(step_index, grad_query):
        offset = step_index * step_rows
        key_block = key_window(key_piece, offset, step_rows, heads_local)
        value_block = key_window(value_piece, offset, step_rows, heads_local)
        positions = offset + jnp.arange(step_rows, dtype=jnp.int32)
        key_live = (positions[None, :] < lengths[:, None])[:, None, None, :]
        probs_low, grad_scores = score_grads(
            queries, grad_heads, key_block, value_block, log_total, row_delta, key_live, score_scale
        )
        return (
            grad_query
            + jnp.einsum(
                "rhqk,rkhd->rqhd", grad_scores, key_block, preferred_element_type=jnp.float32
            )
            * score_scale
        )

    return lax.fori_loop(0, piece_len // step_rows, query_one_step, running)


def key_fold(
    key_heads, value_heads, key_live, stat_logs, stat_deltas, score_scale, running, piece_rows
):
    heads_local = key_heads.shape[2]
    query_piece, grad_piece = piece_rows
    piece_len = query_piece.shape[1]
    step_rows = block_size(piece_len)

    def key_one_step(step_index, loop_state):
        grad_key, grad_value = loop_state
        offset = step_index * step_rows
        query_block = key_window(query_piece, offset, step_rows, heads_local)
        grad_block = key_window(grad_piece, offset, step_rows, heads_local)
        log_block = jnp.transpose(
            lax.dynamic_slice_in_dim(stat_logs, offset, step_rows, 1), (0, 2, 1)
        )
        delta_block = jnp.transpose(
            lax.dynamic_slice_in_dim(stat_deltas, offset, step_rows, 1), (0, 2, 1)
        )
        probs_low, grad_scores = score_grads(
            query_block,
            grad_block,
            key_heads,
            value_heads,
            log_block,
            delta_block,
            key_live,
            score_scale,
        )
        grad_key = (
            grad_key
            + jnp.einsum(
                "rhqk,rqhd->rkhd", grad_scores, query_block, preferred_element_type=jnp.float32
            )
            * score_scale
        )
        grad_value = grad_value + jnp.einsum(
            "rhqk,rqhd->rkhd", probs_low, grad_block, preferred_element_type=jnp.float32
        )
        return (grad_key, grad_value)

    return lax.fori_loop(0, piece_len // step_rows, key_one_step, running)


def body(
    tokens,
    cond,
    lengths,
    ada_weight,
    ada_bias,
    norm1_gain,
    qkv_weight,
    out_weight,
    norm2_gain,
    up_weight,
    up_bias,
    down_weight,
    down_bias,
    out_grad,
):
    full_params = (
        lax.all_gather(ada_weight, ("dp", "blk", "head"), axis=1, tiled=True),
        lax.all_gather(ada_bias, ("dp", "blk", "head"), axis=0, tiled=True),
        lax.all_gather(norm1_gain, ("dp", "blk", "head"), axis=0, tiled=True),
        lax.all_gather(qkv_weight, ("dp", "blk", "head"), axis=1, tiled=True),
        lax.all_gather(out_weight, ("dp", "blk", "head"), axis=1, tiled=True),
        lax.all_gather(norm2_gain, ("dp", "blk", "head"), axis=0, tiled=True),
        lax.all_gather(up_weight, ("dp", "blk", "head"), axis=1, tiled=True),
        lax.all_gather(up_bias, ("dp", "blk", "head"), axis=0, tiled=True),
        lax.all_gather(down_weight, ("dp", "blk", "head"), axis=1, tiled=True),
        lax.all_gather(down_bias, ("dp", "blk", "head"), axis=0, tiled=True),
    )
    (
        ada_full,
        ada_bias_full,
        gain_one,
        qkv_full,
        out_full,
        gain_two,
        up_full,
        up_bias_full,
        down_full,
        down_bias_full,
    ) = full_params
    row_count, tok_count, width = tokens.shape
    head_groups = lax.axis_size("head")
    heads_local = HEADS // head_groups
    local_width = heads_local * HEAD_DIM
    group_rows = tok_count * head_groups
    score_scale = HEAD_DIM ** (-0.5)
    float_type = jnp.float32
    cond_wide = cond.astype(float_type)
    modulation = jnp.dot(cond, ada_full, preferred_element_type=float_type) + ada_bias_full.astype(
        float_type
    )
    pieces = [
        modulation[:, None, part_index * width : (part_index + 1) * width]
        for part_index in range(6)
    ]
    shift_one, scale_one, gate_one, shift_two, scale_two, gate_two = pieces
    seq_index = lax.axis_index("blk") * head_groups + lax.axis_index("head")
    positions = seq_index * tok_count + jnp.arange(tok_count, dtype=jnp.int32)
    slot_live = (positions[None, :] < lengths[:, None]).astype(float_type)[..., None]
    cosine, sine = rotary_tables(positions)
    tokens_wide = tokens.astype(float_type)
    unit_one, inverse_one = normalize(tokens_wide)
    normed_one = unit_one * gain_one.astype(float_type)
    hidden_one = (normed_one * (1.0 + scale_one) + shift_one).astype(jnp.bfloat16)
    projected = jnp.einsum("rtd,de->rte", hidden_one, qkv_full, preferred_element_type=float_type)
    projected = projected.reshape(row_count, tok_count, 3, HEADS, HEAD_DIM)
    turned = jnp.stack(
        [
            rotate(projected[:, :, 0], cosine, sine),
            rotate(projected[:, :, 1], cosine, sine),
            projected[:, :, 2],
        ],
        axis=2,
    ).astype(jnp.bfloat16)
    grouped = lax.all_to_all(
        turned.reshape(row_count, tok_count, 3, head_groups, local_width),
        "head",
        split_axis=3,
        concat_axis=1,
        tiled=True,
    )
    query_heads = grouped[:, :, 0, 0].reshape(row_count, group_rows, heads_local, HEAD_DIM)
    key_heads = grouped[:, :, 1, 0]
    value_heads = grouped[:, :, 2, 0]
    start_state = (
        jnp.full((row_count, heads_local, group_rows), NEG_LARGE, float_type),
        jnp.zeros((row_count, heads_local, group_rows), float_type),
        jnp.zeros((row_count, group_rows, heads_local, HEAD_DIM), float_type),
    )
    row_peak, row_total, summed = attend_fold(
        query_heads,
        lengths,
        score_scale,
        start_state,
        (
            lax.all_gather(key_heads, "blk", axis=1, tiled=True),
            lax.all_gather(value_heads, "blk", axis=1, tiled=True),
        ),
    )
    attended_heads = summed / jnp.transpose(row_total, (0, 2, 1))[..., None]
    log_total = row_peak + jnp.log(row_total)
    attended_low = attended_heads.astype(jnp.bfloat16).reshape(
        row_count, group_rows, 1, local_width
    )
    attended_seq = lax.all_to_all(
        attended_low, "head", split_axis=1, concat_axis=2, tiled=True
    ).reshape(row_count, tok_count, width)
    branch_one = jnp.einsum(
        "rtd,de->rte", attended_seq, out_full, preferred_element_type=float_type
    )
    middle = tokens_wide + gate_one * branch_one
    unit_two, inverse_two = normalize(middle)
    normed_two = unit_two * gain_two.astype(float_type)
    hidden_two = (normed_two * (1.0 + scale_two) + shift_two).astype(jnp.bfloat16)
    inner = jnp.einsum(
        "rtd,df->rtf", hidden_two, up_full, preferred_element_type=float_type
    ) + up_bias_full.astype(float_type)
    activated, gelu_back = jax.vjp(partial(jax.nn.gelu, approximate=True), inner)
    activated_low = activated.astype(jnp.bfloat16)
    branch_two = jnp.einsum(
        "rtf,fd->rtd", activated_low, down_full, preferred_element_type=float_type
    ) + down_bias_full.astype(float_type)
    result = middle + gate_two * branch_two
    again = (
        lax.all_gather(ada_weight, ("dp", "blk", "head"), axis=1, tiled=True),
        lax.all_gather(ada_bias, ("dp", "blk", "head"), axis=0, tiled=True),
        lax.all_gather(norm1_gain, ("dp", "blk", "head"), axis=0, tiled=True),
        lax.all_gather(qkv_weight, ("dp", "blk", "head"), axis=1, tiled=True),
        lax.all_gather(out_weight, ("dp", "blk", "head"), axis=1, tiled=True),
        lax.all_gather(norm2_gain, ("dp", "blk", "head"), axis=0, tiled=True),
        lax.all_gather(up_weight, ("dp", "blk", "head"), axis=1, tiled=True),
        lax.all_gather(up_bias, ("dp", "blk", "head"), axis=0, tiled=True),
        lax.all_gather(down_weight, ("dp", "blk", "head"), axis=1, tiled=True),
        lax.all_gather(down_bias, ("dp", "blk", "head"), axis=0, tiled=True),
    )
    ada_back, gain_one_back, qkv_back, out_back, gain_two_back, up_back, down_back = (
        again[0],
        again[2],
        again[3],
        again[4],
        again[5],
        again[6],
        again[8],
    )
    grad_out = out_grad.astype(float_type) * slot_live
    grad_gate_two = jnp.sum(grad_out * branch_two, axis=1)
    grad_branch_two = (grad_out * gate_two).astype(jnp.bfloat16)
    grad_down = jnp.einsum(
        "rtf,rtd->fd", activated_low, grad_branch_two, preferred_element_type=float_type
    )
    grad_down_bias = jnp.sum(grad_branch_two.astype(float_type), axis=(0, 1))
    grad_activated = jnp.einsum(
        "rtd,fd->rtf", grad_branch_two, down_back, preferred_element_type=float_type
    )
    grad_inner = gelu_back(grad_activated)[0].astype(jnp.bfloat16)
    grad_up = jnp.einsum("rtd,rtf->df", hidden_two, grad_inner, preferred_element_type=float_type)
    grad_up_bias = jnp.sum(grad_inner.astype(float_type), axis=(0, 1))
    grad_hidden_two = jnp.einsum(
        "rtf,df->rtd", grad_inner, up_back, preferred_element_type=float_type
    )
    grad_shift_two = jnp.sum(grad_hidden_two, axis=1)
    grad_scale_two = jnp.sum(grad_hidden_two * normed_two, axis=1)
    grad_normed_two = grad_hidden_two * (1.0 + scale_two)
    grad_gain_two = jnp.sum(grad_normed_two * unit_two, axis=(0, 1))
    grad_middle = grad_out + normalize_back(
        grad_normed_two * gain_two_back.astype(float_type), unit_two, inverse_two
    )
    grad_gate_one = jnp.sum(grad_middle * branch_one, axis=1)
    grad_branch_one = (grad_middle * gate_one).astype(jnp.bfloat16)
    grad_out_proj = jnp.einsum(
        "rtd,rte->de", attended_seq, grad_branch_one, preferred_element_type=float_type
    )
    grad_attended = jnp.einsum(
        "rte,de->rtd", grad_branch_one, out_back, preferred_element_type=float_type
    ).astype(jnp.bfloat16)
    grad_heads = lax.all_to_all(
        grad_attended.reshape(row_count, tok_count, head_groups, local_width),
        "head",
        split_axis=2,
        concat_axis=1,
        tiled=True,
    )
    grad_heads = grad_heads.reshape(row_count, group_rows, heads_local, HEAD_DIM)
    row_delta = jnp.transpose(
        jnp.sum(grad_heads.astype(float_type) * attended_heads, axis=-1), (0, 2, 1)
    )
    zero_heads = jnp.zeros((row_count, group_rows, heads_local, HEAD_DIM), float_type)
    stat_logs, stat_deltas = (
        lax.all_gather(jnp.transpose(log_total, (0, 2, 1)), "blk", axis=1, tiled=True),
        lax.all_gather(jnp.transpose(row_delta, (0, 2, 1)), "blk", axis=1, tiled=True),
    )
    grad_query = query_fold(
        query_heads,
        grad_heads,
        log_total,
        row_delta,
        lengths,
        score_scale,
        zero_heads,
        (
            lax.all_gather(key_heads, "blk", axis=1, tiled=True),
            lax.all_gather(value_heads, "blk", axis=1, tiled=True),
        ),
    )
    key_positions = lax.axis_index("blk") * group_rows + jnp.arange(group_rows, dtype=jnp.int32)
    key_live = (key_positions[None, :] < lengths[:, None])[:, None, None, :]
    key_four = key_heads.reshape(row_count, group_rows, heads_local, HEAD_DIM)
    value_four = value_heads.reshape(row_count, group_rows, heads_local, HEAD_DIM)
    grad_key, grad_value = key_fold(
        key_four,
        value_four,
        key_live,
        stat_logs,
        stat_deltas,
        score_scale,
        (zero_heads, zero_heads),
        (
            lax.all_gather(
                query_heads.reshape(row_count, group_rows, local_width), "blk", axis=1, tiled=True
            ),
            lax.all_gather(
                grad_heads.reshape(row_count, group_rows, local_width), "blk", axis=1, tiled=True
            ),
        ),
    )
    grad_stack = jnp.stack(
        [
            grad_query.reshape(row_count, group_rows, local_width),
            grad_key.reshape(row_count, group_rows, local_width),
            grad_value.reshape(row_count, group_rows, local_width),
        ],
        axis=2,
    ).astype(jnp.bfloat16)
    grad_seq = lax.all_to_all(
        grad_stack.reshape(row_count, group_rows, 3, 1, local_width),
        "head",
        split_axis=1,
        concat_axis=3,
        tiled=True,
    )
    grad_seq = grad_seq.astype(float_type).reshape(row_count, tok_count, 3, HEADS, HEAD_DIM)
    grad_projected = jnp.stack(
        [
            rotate_back(grad_seq[:, :, 0], cosine, sine),
            rotate_back(grad_seq[:, :, 1], cosine, sine),
            grad_seq[:, :, 2],
        ],
        axis=2,
    )
    grad_projected = grad_projected.reshape(row_count, tok_count, 3 * width).astype(jnp.bfloat16)
    grad_qkv = jnp.einsum(
        "rtd,rte->de", hidden_one, grad_projected, preferred_element_type=float_type
    )
    grad_hidden_one = jnp.einsum(
        "rte,de->rtd", grad_projected, qkv_back, preferred_element_type=float_type
    )
    grad_shift_one = jnp.sum(grad_hidden_one, axis=1)
    grad_scale_one = jnp.sum(grad_hidden_one * normed_one, axis=1)
    grad_normed_one = grad_hidden_one * (1.0 + scale_one)
    grad_gain_one = jnp.sum(grad_normed_one * unit_one, axis=(0, 1))
    grad_tokens = grad_middle + normalize_back(
        grad_normed_one * gain_one_back.astype(float_type), unit_one, inverse_one
    )
    grad_modulation = jnp.concatenate(
        [
            grad_shift_one,
            grad_scale_one,
            grad_gate_one,
            grad_shift_two,
            grad_scale_two,
            grad_gate_two,
        ],
        axis=-1,
    )
    grad_ada = jnp.dot(cond_wide.T, grad_modulation, precision=HIGHEST)
    grad_ada_bias = jnp.sum(grad_modulation, axis=0)
    cond_part = jnp.dot(grad_modulation, ada_back.astype(float_type).T, precision=HIGHEST)
    grad_cond = lax.psum(cond_part, ("blk", "head"))
    owned_grads = (
        lax.psum_scatter(grad_ada, ("dp", "blk", "head"), scatter_dimension=1, tiled=True),
        lax.psum_scatter(grad_ada_bias, ("dp", "blk", "head"), scatter_dimension=0, tiled=True),
        lax.psum_scatter(grad_gain_one, ("dp", "blk", "head"), scatter_dimension=0, tiled=True),
        lax.psum_scatter(grad_qkv, ("dp", "blk", "head"), scatter_dimension=1, tiled=True),
        lax.psum_scatter(grad_out_proj, ("dp", "blk", "head"), scatter_dimension=1, tiled=True),
        lax.psum_scatter(grad_gain_two, ("dp", "blk", "head"), scatter_dimension=0, tiled=True),
        lax.psum_scatter(grad_up, ("dp", "blk", "head"), scatter_dimension=1, tiled=True),
        lax.psum_scatter(grad_up_bias, ("dp", "blk", "head"), scatter_dimension=0, tiled=True),
        lax.psum_scatter(grad_down, ("dp", "blk", "head"), scatter_dimension=1, tiled=True),
        lax.psum_scatter(grad_down_bias, ("dp", "blk", "head"), scatter_dimension=0, tiled=True),
    )
    return (
        result.astype(jnp.bfloat16),
        grad_tokens,
        grad_cond,
        owned_grads[0],
        owned_grads[1],
        owned_grads[2],
        owned_grads[3],
        owned_grads[4],
        owned_grads[5],
        owned_grads[6],
        owned_grads[7],
        owned_grads[8],
        owned_grads[9],
    )


def solution(mesh):
    placed = (
        P("dp", ("blk", "head"), None),
        P("dp", None),
        P("dp"),
        P(None, ("dp", "blk", "head")),
        P(("dp", "blk", "head")),
        P(("dp", "blk", "head")),
        P(None, ("dp", "blk", "head")),
        P(None, ("dp", "blk", "head")),
        P(("dp", "blk", "head")),
        P(None, ("dp", "blk", "head")),
        P(("dp", "blk", "head")),
        P(None, ("dp", "blk", "head")),
        P(("dp", "blk", "head")),
        P("dp", ("blk", "head"), None),
    )
    return jax.shard_map(
        body,
        mesh=mesh,
        in_specs=placed,
        out_specs=(
            P("dp", ("blk", "head"), None),
            P("dp", ("blk", "head"), None),
            P("dp", None),
            P(None, ("dp", "blk", "head")),
            P(("dp", "blk", "head")),
            P(("dp", "blk", "head")),
            P(None, ("dp", "blk", "head")),
            P(None, ("dp", "blk", "head")),
            P(("dp", "blk", "head")),
            P(None, ("dp", "blk", "head")),
            P(("dp", "blk", "head")),
            P(None, ("dp", "blk", "head")),
            P(("dp", "blk", "head")),
        ),
        check_vma=False,
    )
```

profile of v0, /device:TPU:0, one launch (start us, length us, event | category | flops | bytes accessed | tf_op | source)
XLA Modules:
  0.0 1101.8 jit_solution(14686581439592586791)
XLA Ops:
  14.2 42.7 %all-reduce.11 = (bf16[4608]{0:T(1024)(128)(2,1)S(1)}, bf16[768]{0:T(1024)(128)(2,1)S(1)}, bf16[768]{0:T(1024)(128)(2,1)}, bf16[3072]{0:T(1024)(128)(2,1)}, bf16[768]{0:T(1024)(128)(2,1)}) all-reduce(bf16[4608]{0:T(1024)(128)(2,1)S(1)} %dynamic-update-slice, ...), channel_id=1, replica_groups=mesh['dp'=4,'blk'=2,'head'=4] {'dp','blk','head'}, use_global_device_ids=true, to_apply=%add | all-reduce | flops 9984 | bytes 39936
  59.5 8.1 all-gather.10.cloned.1.call-done
  67.6 1.7 convolution_reduce_fusion
  70.0 59.5 %all-gather.12.cloned.1.call-done = bf16[768,2304]{0,1:T(8,128)(2,1)} async-done(((bf16[768,72]{0,1:T(8,128)(2,1)}), bf16[768,2304]{0,1:T(8,128)(2,1)}) %all-gather.12.cloned.1.call-update) | async-done | bytes 3538960 | tf_op jit(solution)/shard_map/all_gather | solution.py:219
  129.5 3.4 convolution_bitcast_fusion
  134.6 3.5 all-to-all-start
  138.8 15.4 %all-to-all-done = bf16[1,256,3,4,192]{1,4,2,0,3:T(8,128)(2,1)S(1)} async-done(((bf16[1,256,3,4,192]{1,4,2,0,3:T(8,128)(2,1)}), bf16[1,256,3,4,192]{1,4,2,0,3:T(8,128)(2,1)S(1)}, u32[]{:S(2)}, u32[]{:S(2)}) %all-to-all-start) | async-done | bytes 1179680 | tf_op jit(solution)/shard_map/all_to_all | solution.py:273
  156.1 11.2 %all-gather = bf16[1,2048,1,1,192]{1,4,3,2,0:T(8,128)(2,1)S(1)} all-gather(bf16[1,1024,1,1,192]{1,4,3,2,0:T(8,128)(2,1)S(1)} %get-tuple-element.716), channel_id=2, replica_groups=mesh['dp'=4,'blk'=2,'head'=4] {'blk'}, dimensions={1}, use_global_device_ids=true | all-gather | bytes 1179648 | tf_op jit(solution)/shard_map/all_gather | solution.py:294
  167.3 12.9 %all-gather.1 = bf16[1,2048,1,1,192]{1,4,3,2,0:T(8,128)(2,1)S(1)} all-gather(bf16[1,1024,1,1,192]{1,4,3,2,0:T(8,128)(2,1)S(1)} %get-tuple-element.714), channel_id=3, replica_groups=mesh['dp'=4,'blk'=2,'head'=4] {'blk'}, dimensions={1}, use_global_device_ids=true | all-gather | bytes 1179648 | tf_op jit(solution)/shard_map/all_gather | solution.py:295
  180.2 42.4 %while.48 = (s32[]{:T(128)}, f32[1,3,1024]{2,1,0:T(4,128)S(1)}, f32[1,3,1024]{2,1,0:T(4,128)}, f32[1,1024,3,64]{1,3,2,0:T(8,128)S(1)}, s32[1]{0:T(128)}, /*index...) while((s32[]{:T(128)}, f32[1,3,1024]{2,1,0:T(4,128)S(1)}, ...), condition=%wide.region_5.6_spmd.clone, body=%wide.region_2.5_spmd.clone.sunk | while | flops 846811136 | bytes 92709168 | solution.py:124
  181.5 7.1 bitcast_reduce_fusion.2
  189.3 8.9 fusion.177
  198.3 3.1 fusion.178
  202.7 7.1 bitcast_reduce_fusion.2
  210.6 8.8 fusion.177
  219.4 3.1 fusion.178
  222.6 1.6 fusion.105
  224.1 2.4 copy.93
  227.0 4.8 reduce.46
  231.9 2.6 reshape.834
  234.5 4.0 all-to-all-start.1
  241.5 5.3 all-to-all-done.1
  246.9 2.0 reshape.835
  248.8 2.3 copy.94
  252.3 2.8 fusion.123
  255.9 5.5 convolution_add_fusion
  261.4 57.3 %all-gather.18.cloned.1.call-done = bf16[3072,768]{0,1:T(8,128)(2,1)} async-done(((bf16[3072,24]{0,1:T(8,128)(2,1)}), bf16[3072,768]{0,1:T(8,128)(2,1)}) %all-gather.18.cloned.1.call-update) | async-done | bytes 4718608 | tf_op jit(solution)/shard_map/all_gather | solution.py:224
  318.7 7.5 convert_reduce_fusion
  326.2 2.2 fusion.84
  330.3 3.7 convert_reduce_fusion.2
  336.3 3.5 all-to-all-start.2
  340.5 4.5 all_gather.70
  345.1 11.3 %all-gather.2 = bf16[1,2048,1,1,192]{1,4,3,2,0:T(8,128)(2,1)} all-gather(bf16[1,1024,1,1,192]{1,4,3,2,0:T(8,128)(2,1)S(1)} %bitcast.338), channel_id=4, replica_groups=mesh['dp'=4,'blk'=2,'head'=4] {'blk'}, dimensions={1}, use_global_device_ids=true | all-gather | bytes 1179648 | tf_op jit(solution)/shard_map/all_gather | solution.py:416
  360.5 12.1 %all_gather.71 = bf16[1,2048,192]{1,2,0:T(8,128)(2,1)} all-gather(bf16[1,1024,192]{1,2,0:T(8,128)(2,1)} %reshape_reshape.3), channel_id=1, replica_groups=mesh['dp'=4,'blk'=2,'head'=4] {'blk'}, dimensions={1}, use_global_device_ids=true | all-gather | bytes 1179648 | tf_op jit(solution)/shard_map/all_gather | solution.py:419
  373.7 4.7 all-gather.3
  378.4 52.8 %while.50 = (s32[]{:T(128)}, f32[1,1024,3,64]{1,3,2,0:T(8,128)}, f32[1,1024,3,64]{1,3,2,0:T(8,128)}, bf16[1,2048,192]{1,2,0:T(8,128)(2,1)}, bf16[1,1024,3,64]{1,...) while((s32[]{:T(128)}, f32[1,1024,3,64]{1,3,2,0:T(8,128)}, ...), condition=%wide.region_14.15_spmd.clone, body=%wide.region_13.14_spmd.clone.sunk | while | flops 1643055104 | bytes 46685488 | solution.py:196
  379.6 6.4 fusion.193
  387.8 10.0 fusion.194
  397.8 6.8 fusion.195
  405.8 6.4 fusion.193
  414.0 10.1 fusion.194
  424.1 7.1 fusion.195
  433.6 36.2 %while.49 = (s32[]{:T(128)}, f32[1,1024,3,64]{1,3,2,0:T(8,128)}, bf16[1,2048,192]{1,2,0:T(8,128)(2,1)S(1)}, s32[1]{0:T(128)}, bf16[1,1024,3,64]{1,3,2,0:T(8,128)...) while((s32[]{:T(128)}, f32[1,1024,3,64]{1,3,2,0:T(8,128)}, ...), condition=%wide.region_12.13_spmd.clone, body=%wide.region_11.12_spmd.clone.sunk | while | flops 1227425792 | bytes 30353636 | solution.py:152
  433.9 6.4 fusion.184
  441.5 10.2 fusion.185
  451.7 6.4 fusion.184
  459.3 10.4 fusion.185
  471.1 2.6 copy.100
  473.7 3.6 all-to-all-start.3
  477.4 1.9 fusion.106
  479.4 23.5 %all-to-all-done.3 = bf16[1,1024,3,1,192]{4,2,3,0,1:T(4,128)(2,1)S(1)} async-done(((bf16[1,1024,3,1,192]{4,2,3,0,1:T(4,128)(2,1)}), bf16[1,1024,3,1,192]{4,2,3,0,1:T(4,128)(2,1)S(1)}, u32[]{:S(2)}, u32[]{:S(2)}) %all-to-all-start.3) | async-done | bytes 1179680 | tf_op jit(solution)/shard_map/all_to_all | solution.py:432
  502.9 2.4 copy.101
  505.3 2.7 reshape.793
  511.5 1.4 fusion.82
  513.2 3.0 multiply_bitcast_fusion
  516.6 4.2 fusion.103
  521.9 6.7 fusion.117
  529.5 7.5 fusion.97
  537.8 39.6 %all-reduce.10 = (f32[4608]{0:T(1024)S(1)}, f32[768]{0:T(1024)S(1)}, f32[768]{0:T(1024)S(1)}, f32[3072]{0:T(1024)S(1)}, f32[768]{0:T(1024)S(1)}) all-reduce(f32[4608]{0:T(1024)S(1)} %reduce.37, f32[768]{0:T(1024)S(1)} %get-tuple-element.613, ...), channel_id=7, replica_groups=mesh['dp'=4,'blk'=2,'head'=4] {'dp','blk','head'}, use_global_device_ids=true, to_apply=%region_25.26.clone | all-reduce | flops 9984 | bytes 79872
  581.0 13.2 %psum.7 = f32[1,128]{1,0:T(1,128)} all-reduce(f32[1,128]{1,0:T(1,128)S(1)} %fusion.109), channel_id=1, replica_groups=mesh['dp'=4,'blk'=2,'head'=4] {'blk','head'}, use_global_device_ids=true, to_apply=%region_23.24 | all-reduce | flops 128 | bytes 1024 | tf_op jit(solution)/shard_map/psum | solution.py:476
  595.4 91.3 %reduce-scatter.6.cloned.1.call-done = f32[128,144]{0,1:T(8,128)} async-done(((f32[128,4608]{0,1:T(8,128)}), f32[128,144]{0,1:T(8,128)}) %reduce-scatter.6.cloned.1.call-update) | async-done | bytes 73744 | tf_op jit(solution)/shard_map/reduce_scatter | solution.py:478
  686.7 124.8 %reduce-scatter.8.cloned.1.call-done = f32[768,72]{0,1:T(8,128)} async-done(((f32[768,2304]{0,1:T(8,128)}), f32[768,72]{0,1:T(8,128)}) %reduce-scatter.8.cloned.1.call-update) | async-done | bytes 221200 | tf_op jit(solution)/shard_map/reduce_scatter | solution.py:481
  811.5 141.7 %reduce-scatter.12.cloned.1.call-done = f32[768,96]{0,1:T(8,128)} async-done(((f32[768,3072]{0,1:T(8,128)}), f32[768,96]{0,1:T(8,128)}) %reduce-scatter.12.cloned.1.call-update) | async-done | bytes 294928 | tf_op jit(solution)/shard_map/reduce_scatter | solution.py:484
  953.2 141.5 %reduce-scatter.14.cloned.1.call-done = f32[3072,24]{0,1:T(8,128)} async-done(((f32[3072,768]{0,1:T(8,128)}), f32[3072,24]{0,1:T(8,128)}) %reduce-scatter.14.cloned.1.call-update) | async-done | bytes 294928 | tf_op jit(solution)/shard_map/reduce_scatter | solution.py:486
  (292 shorter events, 57.3 us)
Async XLA Ops:
  7.2 60.4 %all-gather.10.cloned.1.call-start = ((), (), s32[]{:S(2)}) async-start(), calls=%async_computation.9 | async-start | bytes 1216512 | tf_op jit(solution)/shard_map/all_gather | solution.py:216
  7.9 121.6 %all-gather.12.cloned.1.call-start = ((), (), s32[]{:S(2)}) async-start(), calls=%async_computation.10 | async-start | bytes 3649536 | tf_op jit(solution)/shard_map/all_gather | solution.py:219
  8.7 243.6 %all-gather.14.cloned.1.call-start = ((), (), s32[]{:S(2)}) async-start(), calls=%async_computation.11 | async-start | bytes 1216512 | tf_op jit(solution)/shard_map/all_gather | solution.py:220
  9.4 246.5 %all-gather.16.cloned.1.call-start = ((), (), s32[]{:S(2)}) async-start(), calls=%async_computation.12 | async-start | bytes 4866048 | tf_op jit(solution)/shard_map/all_gather | solution.py:222
  56.9 76.0 %copy-start.35 = (f32[768]{0:T(1024)}, f32[768]{0:T(1024)S(1)}, u32[]{:S(2)}) copy-start(f32[768]{0:T(1024)S(1)} %convert_element_type.187) | copy-start | bytes 9220
  58.0 74.9 %copy-start.47 = (f32[256]{0:T(256)}, f32[256]{0:T(256)S(1)}, u32[]{:S(2)}) copy-start(f32[256]{0:T(256)S(1)} %broadcast_multiply_fusion.5) | copy-start | bytes 3076
  59.3 73.6 %copy-start.57 = (f32[256]{0:T(256)}, f32[256]{0:T(256)S(1)}, u32[]{:S(2)}) copy-start(f32[256]{0:T(256)S(1)} %add_rsqrt_fusion.1) | copy-start | bytes 3076
  59.5 73.6 %copy-start.26 = (f32[256,32]{0,1:T(8,128)}, f32[256,32]{0,1:T(8,128)S(1)}, u32[]{:S(2)}) copy-start(f32[256,32]{0,1:T(8,128)S(1)} %get-tuple-element.732) | copy-start | bytes 98308
  59.5 73.6 %copy-start.28 = (f32[256,32]{0,1:T(8,128)}, f32[256,32]{0,1:T(8,128)S(1)}, u32[]{:S(2)}) copy-start(f32[256,32]{0,1:T(8,128)S(1)} %get-tuple-element.733) | copy-start | bytes 98308
  70.0 62.9 %copy-start.37 = (f32[768]{0:T(1024)}, f32[768]{0:T(1024)S(1)}, u32[]{:S(2)}) copy-start(f32[768]{0:T(1024)S(1)} %get-tuple-element.626) | copy-start | bytes 9220
  70.0 63.0 %copy-start.54 = (f32[768]{0:T(1024)}, f32[768]{0:T(1024)S(1)}, u32[]{:S(2)}) copy-start(f32[768]{0:T(1024)S(1)} %get-tuple-element.625) | copy-start | bytes 9220
  134.6 19.6 %all-to-all-start = ((bf16[1,256,3,4,192]{1,4,2,0,3:T(8,128)(2,1)}), bf16[1,256,3,4,192]{1,4,2,0,3:T(8,128)(2,1)S(1)}, u32[]{:S(2)}, u32[]{:S(2)}) async-start(bf16[1,256,3,4,192]{1,4,2,0,3:T(8,128)(2,1)} %pad_maximum_fusion), calls=%async_computation | async-start | bytes 2359296 | tf_op jit(solution)/shard_map/all_to_all | solution.py:273
  138.1 180.5 %all-gather.18.cloned.1.call-start = ((), (), s32[]{:S(2)}) async-start(), calls=%async_computation.13 | async-start | bytes 4866048 | tf_op jit(solution)/shard_map/all_gather | solution.py:224
  156.1 24.1 %copy-start.13 = (bf16[1,1024,1,1,192]{1,4,3,2,0:T(8,128)(2,1)}, bf16[1,1024,1,1,192]{1,4,3,2,0:T(8,128)(2,1)S(1)}, u32[]{:S(2)}) copy-start(bf16[1,1024,1,1,192]{1,4,3,2,0:T(8,128)(2,1)S(1)} %get-tuple-element.714) | copy-start | bytes 1179652
  189.3 8.9 copy-start.17
  189.3 9.0 copy-start
  189.3 9.0 copy-start.21
  198.3 3.1 copy-start.18
  210.5 8.8 copy-start.17
  210.5 8.9 copy-start
  210.5 8.9 copy-start.21
  219.4 3.1 copy-start.18
  224.1 15.0 %copy-start.69 = (bf16[768]{0:T(1024)(128)(2,1)S(1)}, bf16[768]{0:T(1024)(128)(2,1)}, u32[]{:S(2)}) copy-start(bf16[768]{0:T(1024)(128)(2,1)} %get-tuple-element.693) | copy-start | bytes 4612
  224.1 15.6 %copy-start.59 = (bf16[3072]{0:T(1024)(128)(2,1)S(1)}, bf16[3072]{0:T(1024)(128)(2,1)}, u32[]{:S(2)}) copy-start(bf16[3072]{0:T(1024)(128)(2,1)} %get-tuple-element.692) | copy-start | bytes 18436
  224.1 16.2 %copy-start.68 = (bf16[768]{0:T(1024)(128)(2,1)S(1)}, bf16[768]{0:T(1024)(128)(2,1)}, u32[]{:S(2)}) copy-start(bf16[768]{0:T(1024)(128)(2,1)} %get-tuple-element.691) | copy-start | bytes 4612
  231.9 20.4 %copy-start.1 = (bf16[1,256,768]{2,1,0:T(8,128)(2,1)S(1)}, bf16[1,256,768]{2,1,0:T(8,128)(2,1)}, u32[]{:S(2)}) copy-start(bf16[1,256,768]{2,1,0:T(8,128)(2,1)} %param.20) | copy-start | bytes 1179652
  234.5 12.4 %all-to-all-start.1 = ((bf16[4,2,24576]{2,1,0:T(2,128)(2,1)}), bf16[4,2,24576]{2,1,0:T(2,128)(2,1)S(1)}, u32[]{:S(2)}, u32[]{:S(2)}) async-start(bf16[4,2,24576]{2,1,0:T(2,128)(2,1)} %reshape.834), calls=%async_computation.1 | async-start | bytes 786432 | tf_op jit(solution)/shard_map/all_to_all | solution.py:303
  255.0 74.1 %copy-start.5 = (f32[1,256,768]{2,1,0:T(8,128)}, f32[1,256,768]{2,1,0:T(8,128)S(1)}, u32[]{:S(2)}) copy-start(f32[1,256,768]{2,1,0:T(8,128)S(1)} %get-tuple-element.699) | copy-start | bytes 2359300
  255.9 62.8 %copy-start.24 = (bf16[1,256,768]{2,1,0:T(8,128)(2,1)S(1)}, bf16[1,256,768]{2,1,0:T(8,128)(2,1)}, u32[]{:S(2)}) copy-start(bf16[1,256,768]{2,1,0:T(8,128)(2,1)} %param.33) | copy-start | bytes 1179652
  318.6 7.5 copy-start.30
  318.6 7.5 copy-start.32
  318.6 7.5 copy-start.45
  318.6 7.5 copy-start.49
  318.7 7.5 copy-start.71
  326.2 3.0 copy-start.7
  326.2 2.9 copy-start.20
  326.2 4.1 copy-start.72
  330.3 4.6 copy-start.8
  330.3 4.6 copy-start.42
  335.4 37.2 %copy-start.12 = (f32[1,1024,3,64]{1,3,2,0:T(8,128)S(1)}, f32[1,1024,3,64]{1,3,2,0:T(8,128)}, u32[]{:S(2)}) copy-start(f32[1,1024,3,64]{1,3,2,0:T(8,128)} %copy-done.11) | copy-start | bytes 2359300
  336.3 20.0 %all-to-all-start.2 = ((bf16[1,256,4,192]{1,3,0,2:T(8,128)(2,1)}), bf16[1,256,4,192]{1,3,0,2:T(8,128)(2,1)S(1)}, u32[]{:S(2)}, u32[]{:S(2)}) async-start(bf16[1,256,4,192]{1,3,0,2:T(8,128)(2,1)} %bitcast.369), calls=%async_computation.2 | async-start | bytes 786432 | tf_op jit(solution)/shard_map/all_to_all | solution.py:374
  340.5 4.5 copy-start.41
  340.5 32.0 %copy-start.19 = (f32[1,3,1024]{2,1,0:T(4,128)S(1)}, f32[1,3,1024]{2,1,0:T(4,128)}, u32[]{:S(2)}) copy-start(f32[1,3,1024]{2,1,0:T(4,128)} %get-tuple-element.479) | copy-start | bytes 36868
  373.7 4.7 copy-start.39
  379.6 6.4 copy-start.22
  379.6 6.4 copy-start.23
  379.6 8.2 copy-start.14
  405.8 6.4 copy-start.22
  405.8 6.4 copy-start.23
  405.8 8.2 copy-start.14
  433.9 7.6 copy-start.40
  451.7 7.6 copy-start.40
  471.1 6.3 copy-start.70
  471.1 6.3 copy-start.4
  471.1 6.3 copy-start.10
  471.1 6.3 copy-start.43
  473.7 29.2 %all-to-all-start.3 = ((bf16[1,1024,3,1,192]{4,2,3,0,1:T(4,128)(2,1)}), bf16[1,1024,3,1,192]{4,2,3,0,1:T(4,128)(2,1)S(1)}, u32[]{:S(2)}, u32[]{:S(2)}) async-start(bf16[1,1024,3,1,192]{4,2,3,0,1:T(4,128)(2,1)} %copy.100), calls=%async_computation.3 | async-start | bytes 4194304 | tf_op jit(solution)/shard_map/all_to_all | solution.py:432
  477.3 118.0 %reduce-scatter.10.cloned.1.call-start = ((), (), s32[]{:S(2)}) async-start(), calls=%async_computation.16 | async-start | bytes 2433024 | tf_op jit(solution)/shard_map/reduce_scatter | solution.py:482
  479.4 207.3 %reduce-scatter.6.cloned.1.call-start = ((), (), s32[]{:S(2)}) async-start(), calls=%async_computation.14 | async-start | bytes 2433024 | tf_op jit(solution)/shard_map/reduce_scatter | solution.py:478
  512.8 3.7 copy-start.55
  516.2 295.3 %reduce-scatter.8.cloned.1.call-start = ((), (), s32[]{:S(2)}) async-start(), calls=%async_computation.15 | async-start | bytes 7299072 | tf_op jit(solution)/shard_map/reduce_scatter | solution.py:481
  520.8 432.4 %reduce-scatter.12.cloned.1.call-start = ((), (), s32[]{:S(2)}) async-start(), calls=%async_computation.17 | async-start | bytes 9732096 | tf_op jit(solution)/shard_map/reduce_scatter | solution.py:484
  528.6 566.1 %reduce-scatter.14.cloned.1.call-start = ((), (), s32[]{:S(2)}) async-start(), calls=%async_computation.18 | async-start | bytes 9732096 | tf_op jit(solution)/shard_map/reduce_scatter | solution.py:486
  537.1 43.3 %copy-start.9 = (bf16[128,4608]{0,1:T(8,128)(2,1)S(1)}, bf16[128,4608]{0,1:T(8,128)(2,1)}, u32[]{:S(2)}) copy-start(bf16[128,4608]{0,1:T(8,128)(2,1)} %all-gather.10.cloned.1.call-done) | copy-start | bytes 3538948
  (32 other events, 42.3 us)
Sparse Core Ops, SparseCore 0:
  10.9 56.6 all-gather.9
  70.5 58.9 all-gather.11
  132.4 54.1 all-gather.13
  189.4 63.2 all-gather.15
  255.4 63.1 all-gather.17
  483.7 98.4 reduce-scatter.9
  588.0 98.6 reduce-scatter.5
  692.9 118.5 reduce-scatter.7
  818.0 135.1 reduce-scatter.11
  959.5 135.1 reduce-scatter.13
where the time goes:
time: 1110 us; the launch traced here: 1100 us
  waiting for transfers between devices  672 us (61%)
  blocking collectives  152 us (14%)
  matrix products  150 us (14%)
  other arithmetic  51.9 us (5%)
  local copies, waits for them, and re-layouts  44.5 us (4%)
  between operations  16 us (1%)
  starting transfers between devices  15.2 us (1%)
    reduce_scatter x1, waiting for transfers between devices, body(): lax.psum_scatter(grad_up, ('dp', 'blk', 'head'), scatter_dimension=1, til...  142 us
    reduce_scatter x1, waiting for transfers between devices, body(): lax.psum_scatter(grad_down, ('dp', 'blk', 'head'), scatter_dimension=1, t...  141 us
    reduce_scatter x1, waiting for transfers between devices, body(): lax.psum_scatter(grad_qkv, ('dp', 'blk', 'head'), scatter_dimension=1, ti...  125 us
    reduce_scatter x1, waiting for transfers between devices, body(): lax.psum_scatter(grad_ada, ('dp', 'blk', 'head'), scatter_dimension=1, ti...  91.3 us
    unnamed x2, blocking collectives  82.3 us
    all_gather x1, waiting for transfers between devices, body(): lax.all_gather(qkv_weight, ('dp', 'blk', 'head'), axis=1, tiled=True)  59.5 us
    all_gather x1, waiting for transfers between devices, body(): lax.all_gather(down_weight, ('dp', 'blk', 'head'), axis=1, tiled=True)  57.3 us
    dot_general x4, matrix products, score_grads(): jnp.einsum('rqhd,rkhd->rhqk', query_block, key_block, preferred_element_t...  25.5 us
  transfers between devices with their start and end apart: 14, of which 10 were waited for; matrix products, arithmetic and copies ran while one was open for 11% of the time, Pallas kernels for 0%

commit v1 on v0

--- a/solution.py
+++ b/solution.py
@@ -4,7 +4,137 @@
 import jax
 import jax.numpy as jnp
 from jax import lax
+from jax.experimental import pallas as pl
+from jax.experimental.pallas import tpu as pltpu
 from jax.sharding import PartitionSpec as P
+
+AXES=("dp","blk","head")
+MESHID = pl.DeviceIdType.MESH
+
+def log2(n):
+    assert n & (n-1) == 0
+    return n.bit_length()-1
+
+class Topo:
+    def __init__(self, mesh):
+        self.nd, self.nb, self.nh = (mesh.shape[a] for a in AXES)
+        self.n = self.nd*self.nb*self.nh
+        lh, lb, ld = log2(self.nh), log2(self.nb), log2(self.nd)
+        head=list(range(lh)); blk=list(range(lh,lh+lb)); dp=list(range(lh+lb,lh+lb+ld))
+        self.orders = (dp+blk+head[1:]+head[:1], dp+head[1:]+blk+head[:1])
+        self.phases = lh+lb+ld
+    def here(self):
+        return (lax.axis_index("dp")*self.nb+lax.axis_index("blk"))*self.nh+lax.axis_index("head")
+    def coords(self, i):
+        return (i//(self.nb*self.nh), (i//self.nh)%self.nb, i%self.nh)
+    def deltas(self, me, color=None):
+        color = me % 2 if color is None else color
+        d=[]
+        for p in range(self.phases):
+            a,b=self.orders[0][p],self.orders[1][p]
+            da=(1-2*((me//2**a)%2))*2**a
+            if a==b: d.append(da)
+            else:
+                db=(1-2*((me//2**b)%2))*2**b
+                d.append(da+color*(db-da))
+        return d
+
+def gather_kernel(topo, count, *refs):
+    ins=refs[:count]; outs=refs[count:2*count]; send,recv,local=refs[2*count:]
+    me=topo.here(); delta=topo.deltas(me); ph=topo.phases; other=topo.deltas(me,1-me%2)
+    def block(a):
+        b=me
+        use=other if a>>(ph-1)&1 else delta
+        for k in range(ph):
+            if a>>k&1: b=b+use[k]
+        return b
+    partner=[topo.coords(me+d) for d in delta]
+    barrier=pltpu.get_barrier_semaphore()
+    for pr in partner: pl.semaphore_signal(barrier,1,device_id=pr,device_id_type=MESHID)
+    pl.semaphore_wait(barrier,ph)
+    def copy(k,a,p,src):
+        blkid=block(a)
+        arr=a+2**p
+        return pltpu.make_async_remote_copy(src_ref=src if a==0 else outs[k].at[blkid], dst_ref=outs[k].at[blkid],
+            send_sem=send.at[k,arr], recv_sem=recv.at[k,arr], device_id=partner[p], device_id_type=MESHID)
+    sends=[]
+    for k in range(count):
+        for p in range(ph):
+            c=copy(k,0,p,ins[k]); c.start(); sends.append(c)
+    locs=[]
+    for k in range(count):
+        c=pltpu.make_async_copy(ins[k],outs[k].at[me],local.at[k]); c.start(); locs.append(c)
+    for a in range(1,2**ph):
+        top=a.bit_length()-1
+        for k in range(count):
+            blkid=block(a)
+            w=pltpu.make_async_remote_copy(src_ref=outs[k].at[blkid],dst_ref=outs[k].at[blkid],send_sem=send.at[k,a],recv_sem=recv.at[k,a],device_id=partner[top],device_id_type=MESHID)
+            w.wait_recv()
+            for p in range(top+1,ph):
+                c=copy(k,a,p,None); c.start(); sends.append(c)
+    for c in sends: c.wait_send()
+    for c in locs: c.wait()
+
+def gather(topo, arrays, cid):
+    n=topo.n; k=len(arrays)
+    return pl.pallas_call(
+        partial(gather_kernel,topo,k),
+        out_shape=[jax.ShapeDtypeStruct((n,)+a.shape,a.dtype) for a in arrays],
+        in_specs=[pl.BlockSpec(memory_space=pltpu.VMEM)]*k,
+        out_specs=[pl.BlockSpec(memory_space=pl.ANY)]*k,
+        scratch_shapes=[pltpu.SemaphoreType.DMA((k,n)),pltpu.SemaphoreType.DMA((k,n)),pltpu.SemaphoreType.DMA((k,))],
+        compiler_params=pltpu.CompilerParams(collective_id=cid,has_side_effects=True),
+        name="gather%d"%cid)(*arrays)
+
+def reduce_kernel(topo, count, *refs):
+    ins=refs[:count]; outs=refs[count:2*count]; arrs=refs[2*count:3*count]; send,recv=refs[3*count:]
+    me=topo.here(); delta=topo.deltas(me); ph=topo.phases; other=topo.deltas(me,1-me%2)
+    def block(a):
+        b=me
+        use=other if a>>(ph-1)&1 else delta
+        for k in range(ph):
+            if a>>k&1: b=b+use[k]
+        return b
+    partner=[topo.coords(me+d) for d in delta]
+    barrier=pltpu.get_barrier_semaphore()
+    for pr in partner: pl.semaphore_signal(barrier,1,device_id=pr,device_id_type=MESHID)
+    pl.semaphore_wait(barrier,ph)
+    def copy(k,a,src):
+        t=a.bit_length()-1
+        return pltpu.make_async_remote_copy(src_ref=src,dst_ref=arrs[k].at[a],send_sem=send.at[k,a],recv_sem=recv.at[k,a],
+            device_id=partner[t],device_id_type=MESHID)
+    sends=[]
+    half=2**(ph-1)
+    for a in range(2**ph-1,half-1,-1):
+        for k in range(count):
+            c=copy(k,a,ins[k].at[block(a)]); c.start(); sends.append(c)
+    for a in range(half-1,-1,-1):
+        t=a.bit_length()-1
+        for k in range(count):
+            total=ins[k][block(a)].astype(jnp.float32)
+            for p in range(ph-1,t,-1):
+                idx=2**p+a
+                copy(k,idx,arrs[k].at[idx]).wait_recv()
+                total=total+arrs[k][idx].astype(jnp.float32)
+            if a==0:
+                outs[k][...]=total
+            else:
+                slot=arrs[k].at[half+a]
+                slot[...]=total.astype(slot.dtype)
+                c=copy(k,a,slot); c.start(); sends.append(c)
+    for c in sends: c.wait_send()
+
+def reduce_scatter(topo, arrays, cid):
+    n=topo.n; k=len(arrays)
+    return pl.pallas_call(
+        partial(reduce_kernel,topo,k),
+        out_shape=[jax.ShapeDtypeStruct(a.shape[1:],jnp.float32) for a in arrays],
+        in_specs=[pl.BlockSpec(memory_space=pltpu.VMEM)]*k,
+        out_specs=[pl.BlockSpec(memory_space=pltpu.VMEM)]*k,
+        scratch_shapes=[pltpu.VMEM(a.shape,a.dtype) for a in arrays]+[pltpu.SemaphoreType.DMA((k,n)),pltpu.SemaphoreType.DMA((k,n))],
+        compiler_params=pltpu.CompilerParams(collective_id=cid,has_side_effects=True,vmem_limit_bytes=60*2**20),
+        name="reduce%d"%cid)(*arrays)
+
 
 HEADS = 12
 HEAD_DIM = 64
@@ -197,6 +327,7 @@
 
 
 def body(
+    topo,
     tokens,
     cond,
     lengths,
@@ -212,41 +343,45 @@
     down_bias,
     out_grad,
 ):
-    full_params = (
-        lax.all_gather(ada_weight, ("dp", "blk", "head"), axis=1, tiled=True),
-        lax.all_gather(ada_bias, ("dp", "blk", "head"), axis=0, tiled=True),
-        lax.all_gather(norm1_gain, ("dp", "blk", "head"), axis=0, tiled=True),
-        lax.all_gather(qkv_weight, ("dp", "blk", "head"), axis=1, tiled=True),
-        lax.all_gather(out_weight, ("dp", "blk", "head"), axis=1, tiled=True),
-        lax.all_gather(norm2_gain, ("dp", "blk", "head"), axis=0, tiled=True),
-        lax.all_gather(up_weight, ("dp", "blk", "head"), axis=1, tiled=True),
-        lax.all_gather(up_bias, ("dp", "blk", "head"), axis=0, tiled=True),
-        lax.all_gather(down_weight, ("dp", "blk", "head"), axis=1, tiled=True),
-        lax.all_gather(down_bias, ("dp", "blk", "head"), axis=0, tiled=True),
-    )
-    (
-        ada_full,
-        ada_bias_full,
-        gain_one,
-        qkv_full,
-        out_full,
-        gain_two,
-        up_full,
-        up_bias_full,
-        down_full,
-        down_bias_full,
-    ) = full_params
+    devices = topo.n
+    rows_all = topo.nd
+    float_type = jnp.float32
+    cond_all = lax.all_gather(cond, "dp", axis=0, tiled=True)
+    mod_columns = ada_weight.shape[1]
+    mod_own = jnp.dot(cond_all, ada_weight, preferred_element_type=float_type) + ada_bias.astype(
+        float_type
+    )
+    vectors = [norm1_gain, norm2_gain, up_bias, down_bias]
+    small = jnp.concatenate(
+        [mod_own.reshape(-1)] + [v.astype(float_type) for v in vectors]
+    )
+    small_used = small.shape[0]
+    small = jnp.pad(small, (0, -small_used % 1024)).reshape(-1, 128)
+    small_all, qkv_t, out_t, up_t, down_t, ada_t = gather(
+        topo, [small, qkv_weight.T, out_weight.T, up_weight.T, down_weight.T, ada_weight.T], 0
+    )
+    qkv_t = qkv_t.reshape(-1, qkv_t.shape[-1])
+    out_t = out_t.reshape(-1, out_t.shape[-1])
+    up_t = up_t.reshape(-1, up_t.shape[-1])
+    down_t = down_t.reshape(-1, down_t.shape[-1])
+    ada_t = ada_t.reshape(-1, ada_t.shape[-1])
+    small_all = small_all.reshape(devices, -1)
+    mod_all = small_all[:, : rows_all * mod_columns].reshape(devices, rows_all, mod_columns)
+    modulation = lax.dynamic_index_in_dim(
+        mod_all, lax.axis_index("dp"), 1, keepdims=False
+    ).reshape(1, -1)
+    cut = rows_all * mod_columns
+    full_vectors = []
+    for v in vectors:
+        full_vectors.append(small_all[:, cut : cut + v.shape[0]].reshape(-1))
+        cut += v.shape[0]
+    gain_one, gain_two, up_bias_full, down_bias_full = full_vectors
     row_count, tok_count, width = tokens.shape
     head_groups = lax.axis_size("head")
     heads_local = HEADS // head_groups
     local_width = heads_local * HEAD_DIM
     group_rows = tok_count * head_groups
     score_scale = HEAD_DIM ** (-0.5)
-    float_type = jnp.float32
-    cond_wide = cond.astype(float_type)
-    modulation = jnp.dot(cond, ada_full, preferred_element_type=float_type) + ada_bias_full.astype(
-        float_type
-    )
     pieces = [
         modulation[:, None, part_index * width : (part_index + 1) * width]
         for part_index in range(6)
@@ -260,7 +395,7 @@
     unit_one, inverse_one = normalize(tokens_wide)
     normed_one = unit_one * gain_one.astype(float_type)
     hidden_one = (normed_one * (1.0 + scale_one) + shift_one).astype(jnp.bfloat16)
-    projected = jnp.einsum("rtd,de->rte", hidden_one, qkv_full, preferred_element_type=float_type)
+    projected = jnp.einsum("rtd,ed->rte", hidden_one, qkv_t, preferred_element_type=float_type)
     projected = projected.reshape(row_count, tok_count, 3, HEADS, HEAD_DIM)
     turned = jnp.stack(
         [
@@ -304,72 +439,51 @@
         attended_low, "head", split_axis=1, concat_axis=2, tiled=True
     ).reshape(row_count, tok_count, width)
     branch_one = jnp.einsum(
-        "rtd,de->rte", attended_seq, out_full, preferred_element_type=float_type
+        "rtd,ed->rte", attended_seq, out_t, preferred_element_type=float_type
     )
     middle = tokens_wide + gate_one * branch_one
     unit_two, inverse_two = normalize(middle)
     normed_two = unit_two * gain_two.astype(float_type)
     hidden_two = (normed_two * (1.0 + scale_two) + shift_two).astype(jnp.bfloat16)
     inner = jnp.einsum(
-        "rtd,df->rtf", hidden_two, up_full, preferred_element_type=float_type
+        "rtd,fd->rtf", hidden_two, up_t, preferred_element_type=float_type
     ) + up_bias_full.astype(float_type)
     activated, gelu_back = jax.vjp(partial(jax.nn.gelu, approximate=True), inner)
     activated_low = activated.astype(jnp.bfloat16)
     branch_two = jnp.einsum(
-        "rtf,fd->rtd", activated_low, down_full, preferred_element_type=float_type
+        "rtf,df->rtd", activated_low, down_t, preferred_element_type=float_type
     ) + down_bias_full.astype(float_type)
     result = middle + gate_two * branch_two
-    again = (
-        lax.all_gather(ada_weight, ("dp", "blk", "head"), axis=1, tiled=True),
-        lax.all_gather(ada_bias, ("dp", "blk", "head"), axis=0, tiled=True),
-        lax.all_gather(norm1_gain, ("dp", "blk", "head"), axis=0, tiled=True),
-        lax.all_gather(qkv_weight, ("dp", "blk", "head"), axis=1, tiled=True),
-        lax.all_gather(out_weight, ("dp", "blk", "head"), axis=1, tiled=True),
-        lax.all_gather(norm2_gain, ("dp", "blk", "head"), axis=0, tiled=True),
-        lax.all_gather(up_weight, ("dp", "blk", "head"), axis=1, tiled=True),
-        lax.all_gather(up_bias, ("dp", "blk", "head"), axis=0, tiled=True),
-        lax.all_gather(down_weight, ("dp", "blk", "head"), axis=1, tiled=True),
-        lax.all_gather(down_bias, ("dp", "blk", "head"), axis=0, tiled=True),
-    )
-    ada_back, gain_one_back, qkv_back, out_back, gain_two_back, up_back, down_back = (
-        again[0],
-        again[2],
-        again[3],
-        again[4],
-        again[5],
-        again[6],
-        again[8],
-    )
     grad_out = out_grad.astype(float_type) * slot_live
     grad_gate_two = jnp.sum(grad_out * branch_two, axis=1)
     grad_branch_two = (grad_out * gate_two).astype(jnp.bfloat16)
     grad_down = jnp.einsum(
-        "rtf,rtd->fd", activated_low, grad_branch_two, preferred_element_type=float_type
+        "rtd,rtf->df", grad_branch_two, activated_low, preferred_element_type=float_type
     )
     grad_down_bias = jnp.sum(grad_branch_two.astype(float_type), axis=(0, 1))
     grad_activated = jnp.einsum(
-        "rtd,fd->rtf", grad_branch_two, down_back, preferred_element_type=float_type
+        "rtd,df->rtf", grad_branch_two, down_t, preferred_element_type=float_type
     )
     grad_inner = gelu_back(grad_activated)[0].astype(jnp.bfloat16)
-    grad_up = jnp.einsum("rtd,rtf->df", hidden_two, grad_inner, preferred_element_type=float_type)
+    grad_up = jnp.einsum("rtf,rtd->fd", grad_inner, hidden_two, preferred_element_type=float_type)
     grad_up_bias = jnp.sum(grad_inner.astype(float_type), axis=(0, 1))
     grad_hidden_two = jnp.einsum(
-        "rtf,df->rtd", grad_inner, up_back, preferred_element_type=float_type
+        "rtf,fd->rtd", grad_inner, up_t, preferred_element_type=float_type
     )
     grad_shift_two = jnp.sum(grad_hidden_two, axis=1)
     grad_scale_two = jnp.sum(grad_hidden_two * normed_two, axis=1)
     grad_normed_two = grad_hidden_two * (1.0 + scale_two)
     grad_gain_two = jnp.sum(grad_normed_two * unit_two, axis=(0, 1))
     grad_middle = grad_out + normalize_back(
-        grad_normed_two * gain_two_back.astype(float_type), unit_two, inverse_two
+        grad_normed_two * gain_two.astype(float_type), unit_two, inverse_two
     )
     grad_gate_one = jnp.sum(grad_middle * branch_one, axis=1)
     grad_branch_one = (grad_middle * gate_one).astype(jnp.bfloat16)
     grad_out_proj = jnp.einsum(
-        "rtd,rte->de", attended_seq, grad_branch_one, preferred_element_type=float_type
+        "rte,rtd->ed", grad_branch_one, attended_seq, preferred_element_type=float_type
     )
     grad_attended = jnp.einsum(
-        "rte,de->rtd", grad_branch_one, out_back, preferred_element_type=float_type
+        "rte,ed->rtd", grad_branch_one, out_t, preferred_element_type=float_type
     ).astype(jnp.bfloat16)
     grad_heads = lax.all_to_all(
         grad_attended.reshape(row_count, tok_count, head_groups, local_width),
@@ -447,17 +561,17 @@
     )
     grad_projected = grad_projected.reshape(row_count, tok_count, 3 * width).astype(jnp.bfloat16)
     grad_qkv = jnp.einsum(
-        "rtd,rte->de", hidden_one, grad_projected, preferred_element_type=float_type
+        "rte,rtd->ed", grad_projected, hidden_one, preferred_element_type=float_type
     )
     grad_hidden_one = jnp.einsum(
-        "rte,de->rtd", grad_projected, qkv_back, preferred_element_type=float_type
+        "rte,ed->rtd", grad_projected, qkv_t, preferred_element_type=float_type
     )
     grad_shift_one = jnp.sum(grad_hidden_one, axis=1)
     grad_scale_one = jnp.sum(grad_hidden_one * normed_one, axis=1)
     grad_normed_one = grad_hidden_one * (1.0 + scale_one)
     grad_gain_one = jnp.sum(grad_normed_one * unit_one, axis=(0, 1))
     grad_tokens = grad_middle + normalize_back(
-        grad_normed_one * gain_one_back.astype(float_type), unit_one, inverse_one
+        grad_normed_one * gain_one.astype(float_type), unit_one, inverse_one
     )
     grad_modulation = jnp.concatenate(
         [
@@ -470,36 +584,57 @@
         ],
         axis=-1,
     )
-    grad_ada = jnp.dot(cond_wide.T, grad_modulation, precision=HIGHEST)
-    grad_ada_bias = jnp.sum(grad_modulation, axis=0)
-    cond_part = jnp.dot(grad_modulation, ada_back.astype(float_type).T, precision=HIGHEST)
-    grad_cond = lax.psum(cond_part, ("blk", "head"))
-    owned_grads = (
-        lax.psum_scatter(grad_ada, ("dp", "blk", "head"), scatter_dimension=1, tiled=True),
-        lax.psum_scatter(grad_ada_bias, ("dp", "blk", "head"), scatter_dimension=0, tiled=True),
-        lax.psum_scatter(grad_gain_one, ("dp", "blk", "head"), scatter_dimension=0, tiled=True),
-        lax.psum_scatter(grad_qkv, ("dp", "blk", "head"), scatter_dimension=1, tiled=True),
-        lax.psum_scatter(grad_out_proj, ("dp", "blk", "head"), scatter_dimension=1, tiled=True),
-        lax.psum_scatter(grad_gain_two, ("dp", "blk", "head"), scatter_dimension=0, tiled=True),
-        lax.psum_scatter(grad_up, ("dp", "blk", "head"), scatter_dimension=1, tiled=True),
-        lax.psum_scatter(grad_up_bias, ("dp", "blk", "head"), scatter_dimension=0, tiled=True),
-        lax.psum_scatter(grad_down, ("dp", "blk", "head"), scatter_dimension=1, tiled=True),
-        lax.psum_scatter(grad_down_bias, ("dp", "blk", "head"), scatter_dimension=0, tiled=True),
-    )
+    cond_part = jnp.dot(
+        grad_modulation, ada_t.astype(float_type), precision=HIGHEST
+    ).reshape(1, -1)
+    plane = jnp.arange(devices, dtype=jnp.int32) // (topo.nb * topo.nh) == lax.axis_index("dp")
+    row_here = jnp.arange(rows_all, dtype=jnp.int32) == lax.axis_index("dp")
+    mod_blocks = jnp.where(
+        row_here[None, :, None], grad_modulation.reshape(devices, 1, mod_columns), 0.0
+    )
+    small_grads = jnp.concatenate(
+        [mod_blocks.reshape(devices, -1)]
+        + [
+            v.reshape(devices, -1)
+            for v in (grad_gain_one, grad_gain_two, grad_up_bias, grad_down_bias)
+        ]
+        + [jnp.where(plane[:, None], cond_part, 0.0)],
+        axis=1,
+    )
+    used = small_grads.shape[1]
+    small_grads = jnp.pad(small_grads, ((0, 0), (0, -used % 1024))).reshape(devices, -1, 128)
+    small_own, qkv_own, out_own, up_own, down_own = reduce_scatter(
+        topo,
+        [small_grads]
+        + [
+            g.astype(jnp.bfloat16).reshape(devices, -1, g.shape[-1])
+            for g in (grad_qkv, grad_out_proj, grad_up, grad_down)
+        ],
+        1,
+    )
+    small_own = small_own.reshape(-1)
+    mod_grads = small_own[: rows_all * mod_columns].reshape(rows_all, mod_columns)
+    cut = rows_all * mod_columns
+    vector_grads = []
+    for v in vectors:
+        vector_grads.append(small_own[cut : cut + v.shape[0]])
+        cut += v.shape[0]
+    grad_cond = small_own[cut : cut + cond.shape[1]].reshape(1, -1)
+    grad_ada = jnp.dot(cond_all.astype(float_type).T, mod_grads, precision=HIGHEST)
     return (
         result.astype(jnp.bfloat16),
         grad_tokens,
         grad_cond,
-        owned_grads[0],
-        owned_grads[1],
-        owned_grads[2],
-        owned_grads[3],
-        owned_grads[4],
-        owned_grads[5],
-        owned_grads[6],
-        owned_grads[7],
-        owned_grads[8],
-        owned_grads[9],
+        grad_ada,
+        jnp.sum(mod_grads, axis=0),
+        vector_grads[0],
+        qkv_own.T,
+        out_own.T,
+        vector_grads[1],
+        up_own.T,
+        vector_grads[2],
+        down_own.T,
+        vector_grads[3],
     )
 
 
@@ -521,7 +656,7 @@
         P("dp", ("blk", "head"), None),
     )
     return jax.shard_map(
-        body,
+        partial(body, Topo(mesh)),
         mesh=mesh,
         in_specs=placed,
         out_specs=(

time: 1110 us -> 527 us (0.47)
  waiting for transfers between devices: 672 us -> 32 us
  Pallas kernels: 0 us -> 169 us
  blocking collectives: 152 us -> 67.2 us
  between operations: 16 us -> 2.78 us
    reduce_scatter x5 -> x0, waiting for transfers between devices: 499 us -> none  [the longest x1 142 us: body(): lax.psum_scatter(grad_up, ('dp', 'blk', 'head'), scatter_dimension=1, til...]
    pallas_call x0 -> x2, Pallas kernels: none -> 169 us  [the longest x1 93.5 us: reduce_scatter(): pl.pallas_call(partial(reduce_kernel, topo, k), out_shape=[jax.ShapeDtype...]
    all_gather x5 -> x0, waiting for transfers between devices: 125 us -> none  [the longest x1 59.5 us: body(): lax.all_gather(qkv_weight, ('dp', 'blk', 'head'), axis=1, tiled=True)]
    unnamed x2 -> x0, blocking collectives: 82.3 us -> none
    psum x1 -> x0, blocking collectives: 13.2 us -> none  [body(): grad_cond = lax.psum(cond_part, ('blk', 'head'))]
    all_gather x0 -> x1, blocking collectives: none -> 12.8 us  [body(): cond_all = lax.all_gather(cond, 'dp', axis=0, tiled=True)]
    dot_general x14 -> x15, matrix products: 49.4 us -> 39 us  [the longest x1 5.29 us: body(): jnp.einsum('rtf,rtd->fd', grad_inner, hidden_two, preferred_element_type=...]
  transfers between devices with their start and end apart: 14 -> 4, of which waited for: 10 -> 3; matrix products, arithmetic and copies ran while one was open for 11% -> 3% of each run, Pallas kernels for 0% -> 0%
where the time goes in v1:
time: 527 us; the launch traced here: 520 us
  Pallas kernels  169 us (32%)
  matrix products  139 us (26%)
  blocking collectives  67.2 us (13%)
  other arithmetic  48.3 us (9%)
  local copies, waits for them, and re-layouts  47.1 us (9%)
  waiting for transfers between devices  32 us (6%)
  starting transfers between devices  14.4 us (3%)
    pallas_call x1, Pallas kernels, reduce_scatter(): pl.pallas_call(partial(reduce_kernel, topo, k), out_shape=[jax.ShapeDtype...  93.5 us
    pallas_call x1, Pallas kernels, gather(): pl.pallas_call(partial(gather_kernel, topo, k), out_shape=[jax.ShapeDtype...  75.2 us
    dot_general x4, matrix products, score_grads(): jnp.einsum('rqhd,rkhd->rhqk', query_block, key_block, preferred_element_t...  25.4 us
    dot_general x2, matrix products, query_one_step(): jnp.einsum('rhqk,rkhd->rqhd', grad_scores, key_block, preferred_element_t...  20.6 us
    dot_general x2, matrix products, key_one_step(): jnp.einsum('rhqk,rqhd->rkhd', grad_scores, query_block, preferred_element...  20.2 us
    reduce_sum x2, other arithmetic, attend_one_step(): row_total = row_total * fade_factor + jnp.sum(weights, axis=-1)  17.4 us
    dot_general x2, matrix products, attend_one_step(): jnp.einsum('rqhd,rkhd->rhqk', queries, key_block, preferred_element_type=...  14.2 us
    unnamed x161, local copies, waits for them, and re-layouts  14 us
  transfers between devices with their start and end apart: 4, of which 3 were waited for; matrix products, arithmetic and copies ran while one was open for 3% of the time, Pallas kernels for 0%

profile of v1, /device:TPU:0, one launch (start us, length us, event | category | flops | bytes accessed | tf_op | source)
XLA Modules:
  0.0 520.3 jit_solution(4898418538120344518)
XLA Ops:
  1.3 12.8 %all-gather.4 = bf16[4,1,128]{2,1,0:T(2,128)(2,1)S(1)} all-gather(bf16[1,1,128]{2,1,0:T(2,128)(2,1)} %bitcast.437), channel_id=1, replica_groups=mesh['dp'=4,'blk'=2,'head'=4] {'dp'}, dimensions={0}, use_global_device_ids=true | all-gather | bytes 1280 | tf_op jit(solution)/shard_map/all_gather | solution.py:349
  15.7 2.8 concatenate.52
  19.0 75.2 %gather0.1 = (f32[32,8,128]{2,1,0:T(8,128)}, bf16[32,72,768]{2,1,0:T(8,128)(2,1)}, bf16[32,24,768]{2,1,0:T(8,128)(2,1)}, bf16[32,96,768]{2,1,0:T(8,128)(2,1)}, b...) custom-call(f32[8,128]{1,0:T(8,128)} %pad_bitcast_fusion.1.refs_0_, bf16[72,768]{1,0:T(8,128)(2,1)} %bitcast.426, ...), custom_call_target="tpu_custom_call" | custom-call | tf_op jit(solution)/shard_map/gather0/pallas_call | solution.py:80
  97.5 1.2 fusion.83
  98.8 3.4 convolution_bitcast_fusion
  104.4 3.5 all-to-all-start
  110.7 13.0 %all-to-all-done = bf16[1,256,3,4,192]{1,4,2,0,3:T(8,128)(2,1)S(1)} async-done(((bf16[1,256,3,4,192]{1,4,2,0,3:T(8,128)(2,1)}), bf16[1,256,3,4,192]{1,4,2,0,3:T(8,128)(2,1)S(1)}, u32[]{:S(2)}, u32[]{:S(2)}) %all-to-all-start) | async-done | bytes 1179680 | tf_op jit(solution)/shard_map/all_to_all | solution.py:408
  125.6 11.2 %all-gather = bf16[1,2048,1,1,192]{1,4,3,2,0:T(8,128)(2,1)S(1)} all-gather(bf16[1,1024,1,1,192]{1,4,3,2,0:T(8,128)(2,1)S(1)} %get-tuple-element.728), channel_id=2, replica_groups=mesh['dp'=4,'blk'=2,'head'=4] {'blk'}, dimensions={1}, use_global_device_ids=true | all-gather | bytes 1179648 | tf_op jit(solution)/shard_map/all_gather | solution.py:429
  136.9 10.5 %all-gather.1 = bf16[1,2048,1,1,192]{1,4,3,2,0:T(8,128)(2,1)S(1)} all-gather(bf16[1,1024,1,1,192]{1,4,3,2,0:T(8,128)(2,1)S(1)} %get-tuple-element.726), channel_id=3, replica_groups=mesh['dp'=4,'blk'=2,'head'=4] {'blk'}, dimensions={1}, use_global_device_ids=true | all-gather | bytes 1179648 | tf_op jit(solution)/shard_map/all_gather | solution.py:430
  147.4 42.0 %while.48 = (s32[]{:T(128)}, f32[1,3,1024]{2,1,0:T(4,128)S(1)}, f32[1,3,1024]{2,1,0:T(4,128)}, f32[1,1024,3,64]{1,3,2,0:T(8,128)S(1)}, s32[1]{0:T(128)}, /*index...) while((s32[]{:T(128)}, f32[1,3,1024]{2,1,0:T(4,128)S(1)}, ...), condition=%wide.region_5.6_spmd.clone, body=%wide.region_2.5_spmd.clone.sunk | while | flops 846811136 | bytes 92709168 | solution.py:254
  147.4 1.2 add_compare_fusion.4
  148.7 7.1 %bitcast_reduce_fusion.2 = (f32[3,1024]{1,0:T(4,128)}, f32[3,1024,1024]{2,1,0:T(8,128)}) fusion(pred[1024]{0:T(1024)(128)(4,1)} %add_compare_fusion.4, bf16[1024,3,64]{0,2,1:T(8,128)(2,1)S(1)} %bitcast.372, bf16[1,1024,3,64]{1,3,2,0:T(8,128)(2,1)S(1)} %get-tuple-element.984), kind=kOutput, calls=%fused_computation.2.clone.1 | convolution fusion | flops 412087296 | bytes 13382656 | tf_op jit(solution)/shard_map/while/body/eval_jaxpr/rqhd,rkhd->rhqk/dot_general | solution.py:237
  156.5 8.7 %fusion.179 = f32[3,1024]{1,0:T(4,128)S(1)} fusion(f32[3,1024,1024]{2,1,0:T(8,128)} %get-tuple-element.925, f32[3,1024]{1,0:T(4,128)S(1)} %bitcast.386, pred[1024]{0:T(1024)(128)(4,1)} %add_compare_fusion.4), kind=kLoop, calls=%fused_computation.7.clone.1 | loop fusion | flops 15725568 | bytes 12608512 | tf_op jit(solution)/shard_map/while/body/eval_jaxpr/reduce_sum | solution.py:244
  165.3 3.1 fusion.180
  168.4 1.2 add_compare_fusion.4
  169.7 7.1 %bitcast_reduce_fusion.2 = (f32[3,1024]{1,0:T(4,128)}, f32[3,1024,1024]{2,1,0:T(8,128)}) fusion(pred[1024]{0:T(1024)(128)(4,1)} %add_compare_fusion.4, bf16[1024,3,64]{0,2,1:T(8,128)(2,1)S(1)} %bitcast.372, bf16[1,1024,3,64]{1,3,2,0:T(8,128)(2,1)S(1)} %get-tuple-element.984), kind=kOutput, calls=%fused_computation.2.clone.1 | convolution fusion | flops 412087296 | bytes 13382656 | tf_op jit(solution)/shard_map/while/body/eval_jaxpr/rqhd,rkhd->rhqk/dot_general | solution.py:237
  177.5 8.7 %fusion.179 = f32[3,1024]{1,0:T(4,128)S(1)} fusion(f32[3,1024,1024]{2,1,0:T(8,128)} %get-tuple-element.925, f32[3,1024]{1,0:T(4,128)S(1)} %bitcast.386, pred[1024]{0:T(1024)(128)(4,1)} %add_compare_fusion.4), kind=kLoop, calls=%fused_computation.7.clone.1 | loop fusion | flops 15725568 | bytes 12608512 | tf_op jit(solution)/shard_map/while/body/eval_jaxpr/reduce_sum | solution.py:244
  186.3 3.1 fusion.180
  189.4 1.6 fusion.103
  191.0 2.4 copy.93
  193.9 4.8 reduce.46
  198.7 2.5 reshape.932
  201.2 3.7 all-to-all-start.1
  206.7 5.6 %all-to-all-done.1 = bf16[4,2,24576]{2,1,0:T(2,128)(2,1)S(1)} async-done(((bf16[4,2,24576]{2,1,0:T(2,128)(2,1)}), bf16[4,2,24576]{2,1,0:T(2,128)(2,1)S(1)}, u32[]{:S(2)}, u32[]{:S(2)}) %all-to-all-start.1) | async-done | bytes 393248 | tf_op jit(solution)/shard_map/all_to_all | solution.py:438
  212.2 2.0 reshape.933
  214.2 2.3 copy.94
  216.9 2.1 fusion.122
  219.4 3.9 convolution_add_fusion
  223.4 4.6 convert_reduce_fusion
  228.0 2.2 fusion.84
  230.9 3.8 convert_reduce_fusion.2
  237.0 3.5 all-to-all-start.2
  241.2 4.5 all_gather.27
  245.7 11.3 %all-gather.2 = bf16[1,2048,1,1,192]{1,4,3,2,0:T(8,128)(2,1)} all-gather(bf16[1,1024,1,1,192]{1,4,3,2,0:T(8,128)(2,1)S(1)} %bitcast.367), channel_id=4, replica_groups=mesh['dp'=4,'blk'=2,'head'=4] {'blk'}, dimensions={1}, use_global_device_ids=true | all-gather | bytes 1179648 | tf_op jit(solution)/shard_map/all_gather | solution.py:530
  257.8 1.3 copy.98
  261.1 11.9 %all_gather.28 = bf16[1,2048,192]{1,2,0:T(8,128)(2,1)} all-gather(bf16[1,1024,192]{1,2,0:T(8,128)(2,1)} %reshape_reshape.3), channel_id=1, replica_groups=mesh['dp'=4,'blk'=2,'head'=4] {'blk'}, dimensions={1}, use_global_device_ids=true | all-gather | bytes 1179648 | tf_op jit(solution)/shard_map/all_gather | solution.py:533
  274.2 4.9 all-gather.3
  279.1 52.8 %while.50 = (s32[]{:T(128)}, f32[1,1024,3,64]{1,3,2,0:T(8,128)}, f32[1,1024,3,64]{1,3,2,0:T(8,128)}, bf16[1,2048,192]{1,2,0:T(8,128)(2,1)}, bf16[1,1024,3,64]{1,...) while((s32[]{:T(128)}, f32[1,1024,3,64]{1,3,2,0:T(8,128)}, ...), condition=%wide.region_14.15_spmd.clone, body=%wide.region_13.14_spmd.clone.sunk | while | flops 1643055104 | bytes 46685488 | solution.py:326
  280.3 6.4 %fusion.195 = f32[3,1024,1024]{2,1,0:T(8,128)} fusion(bf16[1024,3,64]{0,2,1:T(8,128)(2,1)S(1)} %bitcast.368, bf16[1,1024,3,64]{1,3,2,0:T(8,128)(2,1)S(1)} %get-tuple-element.1024), kind=kOutput, calls=%fused_computation.56.clone.1 | convolution fusion | flops 402653184 | bytes 13369344 | tf_op jit(solution)/shard_map/while/body/eval_jaxpr/rqhd,rkhd->rhqk/dot_general | solution.py:212
  287.3 1.2 compare_reduce_fusion.2
  288.5 10.0 %fusion.196 = f32[1,1024,3,64]{1,3,2,0:T(8,128)} fusion(bf16[1024,3,64]{0,2,1:T(8,128)(2,1)S(1)} %bitcast.369, f32[3,1024,1024]{2,1,0:T(8,128)} %fusion.195, f32[3,1024]{1,0:T(4,128)} %get-tuple-element.951, f32[3,1024]{1,0:T(4,128)S(1)} %get-tuple-element.952, pred[1024]{0:T(1024)(128)(4,1)} %compare_reduce_fusion.2, ...), kind=kOutput, calls=%fused_computation.53.clone.1 | convolution fusion | flops 824770560 | bytes 15361025 | tf_op jit(solution)/shard_map/while/body/eval_jaxpr/rhqk,rqhd->rkhd/dot_general | solution.py:316
  298.5 6.8 %fusion.197 = f32[1,1024,3,64]{1,3,2,0:T(8,128)} fusion(bf16[1024,3,64]{0,2,1:T(8,128)(2,1)S(1)} %bitcast.380, f32[3,1024,1024]{2,1,0:T(8,128)} %fusion.195, f32[3,1024]{1,0:T(4,128)S(1)} %get-tuple-element.952, pred[1024]{0:T(1024)(128)(4,1)} %compare_reduce_fusion.2, f32[1,1024,3,64]{1,3,2,0:T(8,128)} %get-tuple-element.1007, pred[]{:T(512)S(6)} %compare.17), kind=kOutput, calls=%fused_computation.54.clone.1 | convolution fusion | flops 415629312 | bytes 14562305 | tf_op jit(solution)/shard_map/while/body/eval_jaxpr/rhqk,rqhd->rkhd/dot_general | solution.py:321
  306.5 6.3 %fusion.195 = f32[3,1024,1024]{2,1,0:T(8,128)} fusion(bf16[1024,3,64]{0,2,1:T(8,128)(2,1)S(1)} %bitcast.368, bf16[1,1024,3,64]{1,3,2,0:T(8,128)(2,1)S(1)} %get-tuple-element.1024), kind=kOutput, calls=%fused_computation.56.clone.1 | convolution fusion | flops 402653184 | bytes 13369344 | tf_op jit(solution)/shard_map/while/body/eval_jaxpr/rqhd,rkhd->rhqk/dot_general | solution.py:212
  314.7 10.1 %fusion.196 = f32[1,1024,3,64]{1,3,2,0:T(8,128)} fusion(bf16[1024,3,64]{0,2,1:T(8,128)(2,1)S(1)} %bitcast.369, f32[3,1024,1024]{2,1,0:T(8,128)} %fusion.195, f32[3,1024]{1,0:T(4,128)} %get-tuple-element.951, f32[3,1024]{1,0:T(4,128)S(1)} %get-tuple-element.952, pred[1024]{0:T(1024)(128)(4,1)} %compare_reduce_fusion.2, ...), kind=kOutput, calls=%fused_computation.53.clone.1 | convolution fusion | flops 824770560 | bytes 15361025 | tf_op jit(solution)/shard_map/while/body/eval_jaxpr/rhqk,rqhd->rkhd/dot_general | solution.py:316
  324.9 7.1 %fusion.197 = f32[1,1024,3,64]{1,3,2,0:T(8,128)} fusion(bf16[1024,3,64]{0,2,1:T(8,128)(2,1)S(1)} %bitcast.380, f32[3,1024,1024]{2,1,0:T(8,128)} %fusion.195, f32[3,1024]{1,0:T(4,128)S(1)} %get-tuple-element.952, pred[1024]{0:T(1024)(128)(4,1)} %compare_reduce_fusion.2, f32[1,1024,3,64]{1,3,2,0:T(8,128)} %get-tuple-element.1007, pred[]{:T(512)S(6)} %compare.17), kind=kOutput, calls=%fused_computation.54.clone.1 | convolution fusion | flops 415629312 | bytes 14562305 | tf_op jit(solution)/shard_map/while/body/eval_jaxpr/rhqk,rqhd->rkhd/dot_general | solution.py:321
  334.3 36.1 %while.49 = (s32[]{:T(128)}, f32[1,1024,3,64]{1,3,2,0:T(8,128)}, bf16[1,2048,192]{1,2,0:T(8,128)(2,1)S(1)}, s32[1]{0:T(128)}, bf16[1,1024,3,64]{1,3,2,0:T(8,128)...) while((s32[]{:T(128)}, f32[1,1024,3,64]{1,3,2,0:T(8,128)}, ...), condition=%wide.region_12.13_spmd.clone, body=%wide.region_11.12_spmd.clone.sunk | while | flops 1227425792 | bytes 30353636 | solution.py:282
  334.6 6.4 %fusion.186 = f32[3,1024,1024]{2,1,0:T(8,128)} fusion(bf16[1024,3,64]{0,2,1:T(8,128)(2,1)S(1)} %bitcast.370, bf16[1,1024,3,64]{1,3,2,0:T(8,128)(2,1)S(1)} %get-tuple-element.1065), kind=kOutput, calls=%fused_computation.35.clone.1 | convolution fusion | flops 402653184 | bytes 13369344 | tf_op jit(solution)/shard_map/while/body/eval_jaxpr/rqhd,rkhd->rhqk/dot_general | solution.py:212
  342.2 10.2 %fusion.187 = f32[1,1024,3,64]{1,3,2,0:T(8,128)} fusion(bf16[1024,3,64]{0,2,1:T(8,128)(2,1)S(1)} %bitcast.371, f32[3,1024,1024]{2,1,0:T(8,128)} %fusion.186, f32[3,1024]{1,0:T(4,128)S(1)} %bitcast.429, f32[3,1024]{1,0:T(4,128)} %bitcast.431, pred[1024]{0:T(1024)(128)(4,1)} %add_compare_fusion.5, bf16[1024,3,64]{0,2,1:T(8,128)(2,1)S(1)} %bitcast.381, ...), kind=kOutput, calls=%fused_computation.33.clone.1 | convolution fusion | flops 824770560 | bytes 15361025 | tf_op jit(solution)/shard_map/while/body/eval_jaxpr/rhqk,rkhd->rqhd/dot_general | solution.py:276
  352.4 6.4 %fusion.186 = f32[3,1024,1024]{2,1,0:T(8,128)} fusion(bf16[1024,3,64]{0,2,1:T(8,128)(2,1)S(1)} %bitcast.370, bf16[1,1024,3,64]{1,3,2,0:T(8,128)(2,1)S(1)} %get-tuple-element.1065), kind=kOutput, calls=%fused_computation.35.clone.1 | convolution fusion | flops 402653184 | bytes 13369344 | tf_op jit(solution)/shard_map/while/body/eval_jaxpr/rqhd,rkhd->rhqk/dot_general | solution.py:212
  360.0 10.4 %fusion.187 = f32[1,1024,3,64]{1,3,2,0:T(8,128)} fusion(bf16[1024,3,64]{0,2,1:T(8,128)(2,1)S(1)} %bitcast.371, f32[3,1024,1024]{2,1,0:T(8,128)} %fusion.186, f32[3,1024]{1,0:T(4,128)S(1)} %bitcast.429, f32[3,1024]{1,0:T(4,128)} %bitcast.431, pred[1024]{0:T(1024)(128)(4,1)} %add_compare_fusion.5, bf16[1024,3,64]{0,2,1:T(8,128)(2,1)S(1)} %bitcast.381, ...), kind=kOutput, calls=%fused_computation.33.clone.1 | convolution fusion | flops 824770560 | bytes 15361025 | tf_op jit(solution)/shard_map/while/body/eval_jaxpr/rhqk,rkhd->rqhd/dot_general | solution.py:276
  371.8 2.5 copy.100
  374.4 3.8 all-to-all-start.3
  378.2 2.7 convolution_convert_fusion.3
  381.2 5.3 %convolution_convert_fusion.1 = bf16[3072,768]{1,0:T(8,128)(2,1)} fusion(bf16[256,3072]{1,0:T(8,128)(2,1)} %copy-done.8, f32[1,256,768]{2,1,0:T(8,128)S(1)} %copy-done.4, f32[768]{0:T(1024)S(1)} %copy-done.47, f32[768]{0:T(1024)S(1)} %copy-done.42, f32[768]{0:T(1024)S(1)} %copy-done.40, f32[256]{0:T(256)S(1)} %copy-done.60, f32[256]{0:T(256)S(1)} %copy-done.53), kind=kOutput, calls=%fused_computation.68 | convolution fusion | flops 1211498496 | bytes 7089152 | tf_op jit(solution)/shard_map/rtf,rtd->fd/dot_general | solution.py:468
  386.5 3.9 convolution_convert_fusion
  390.4 13.4 %all-to-all-done.3 = bf16[1,1024,3,1,192]{4,2,3,0,1:T(4,128)(2,1)S(1)} async-done(((bf16[1,1024,3,1,192]{4,2,3,0,1:T(4,128)(2,1)}), bf16[1,1024,3,1,192]{4,2,3,0,1:T(4,128)(2,1)S(1)}, u32[]{:S(2)}, u32[]{:S(2)}) %all-to-all-start.3) | async-done | bytes 1179680 | tf_op jit(solution)/shard_map/all_to_all | solution.py:546
  403.8 3.0 copy.105
  408.8 3.1 convolution_convert_fusion.2
  411.9 1.4 fusion.82
  415.5 93.5 %reduce1.1 = (f32[8,128]{1,0:T(8,128)}, f32[72,768]{1,0:T(8,128)}, f32[24,768]{1,0:T(8,128)}, f32[96,768]{1,0:T(8,128)}, f32[24,3072]{1,0:T(8,128)}) custom-call(f32[32,8,128]{2,1,0:T(8,128)} %bitcast.417, bf16[32,72,768]{2,1,0:T(8,128)(2,1)} %bitcast.377, bf16[32,24,768]{2,1,0:T(8,128)(2,1)} %bitcast.390, bf16[32,96,768]{2,1,0:T(8,128)(2,1)} %bitcast.373, ...), custom_call_target="tpu_custom_call" | custom-call | tf_op jit(solution)/shard_map/reduce1/pallas_call | solution.py:129
  509.0 1.3 slice_bitcast_fusion.4
  510.3 1.4 fusion.125
  511.7 1.3 slice.136
  516.4 1.6 copy.156
  (296 shorter events, 45.3 us)
Async XLA Ops:
  96.3 5.9 %copy-start.32 = (f32[768]{0:T(1024)}, f32[768]{0:T(1024)S(1)}, u32[]{:S(2)}) copy-start(f32[768]{0:T(1024)S(1)} %get-tuple-element.648) | copy-start | bytes 9220
  96.3 5.9 %copy-start.44 = (f32[768]{0:T(1024)}, f32[768]{0:T(1024)S(1)}, u32[]{:S(2)}) copy-start(f32[768]{0:T(1024)S(1)} %get-tuple-element.647) | copy-start | bytes 9220
  96.4 5.8 %copy-start.30 = (f32[768]{0:T(1024)}, f32[768]{0:T(1024)S(1)}, u32[]{:S(2)}) copy-start(f32[768]{0:T(1024)S(1)} %mul.526) | copy-start | bytes 9220
  97.5 4.7 copy-start.48
  98.8 3.5 copy-start.54
  104.4 19.3 %all-to-all-start = ((bf16[1,256,3,4,192]{1,4,2,0,3:T(8,128)(2,1)}), bf16[1,256,3,4,192]{1,4,2,0,3:T(8,128)(2,1)S(1)}, u32[]{:S(2)}, u32[]{:S(2)}) async-start(bf16[1,256,3,4,192]{1,4,2,0,3:T(8,128)(2,1)} %pad_maximum_fusion), calls=%async_computation | async-start | bytes 2359296 | tf_op jit(solution)/shard_map/all_to_all | solution.py:408
  125.6 21.8 %copy-start.13 = (bf16[1,1024,1,1,192]{1,4,3,2,0:T(8,128)(2,1)}, bf16[1,1024,1,1,192]{1,4,3,2,0:T(8,128)(2,1)S(1)}, u32[]{:S(2)}) copy-start(bf16[1,1024,1,1,192]{1,4,3,2,0:T(8,128)(2,1)S(1)} %get-tuple-element.726) | copy-start | bytes 1179652
  156.5 8.7 %copy-start.17 = (f32[1,3,1024]{2,1,0:T(4,128)S(1)}, f32[1,3,1024]{2,1,0:T(4,128)}, u32[]{:S(2)}) copy-start(f32[1,3,1024]{2,1,0:T(4,128)} %get-tuple-element.968) | copy-start | bytes 36868 | tf_op jit(solution)/shard_map/while
  156.5 8.8 %copy-start = (f32[3,1024,1024]{2,1,0:T(8,128)S(1)}, f32[3,1024,1024]{2,1,0:T(8,128)}, u32[]{:S(2)}) copy-start(f32[3,1024,1024]{2,1,0:T(8,128)} %get-tuple-element.925) | copy-start | bytes 37748740 | tf_op jit(solution)/shard_map/while
  156.5 8.8 %copy-start.20 = (pred[1024]{0:T(1024)(128)(4,1)S(1)}, pred[1024]{0:T(1024)(128)(4,1)}, u32[]{:S(2)}) copy-start(pred[1024]{0:T(1024)(128)(4,1)} %add_compare_fusion.4) | copy-start | bytes 3076 | tf_op jit(solution)/shard_map/while
  165.3 3.1 copy-start.18
  177.5 8.7 %copy-start.17 = (f32[1,3,1024]{2,1,0:T(4,128)S(1)}, f32[1,3,1024]{2,1,0:T(4,128)}, u32[]{:S(2)}) copy-start(f32[1,3,1024]{2,1,0:T(4,128)} %get-tuple-element.968) | copy-start | bytes 36868 | tf_op jit(solution)/shard_map/while
  177.5 8.8 %copy-start = (f32[3,1024,1024]{2,1,0:T(8,128)S(1)}, f32[3,1024,1024]{2,1,0:T(8,128)}, u32[]{:S(2)}) copy-start(f32[3,1024,1024]{2,1,0:T(8,128)} %get-tuple-element.925) | copy-start | bytes 37748740 | tf_op jit(solution)/shard_map/while
  177.5 8.8 %copy-start.20 = (pred[1024]{0:T(1024)(128)(4,1)S(1)}, pred[1024]{0:T(1024)(128)(4,1)}, u32[]{:S(2)}) copy-start(pred[1024]{0:T(1024)(128)(4,1)} %add_compare_fusion.4) | copy-start | bytes 3076 | tf_op jit(solution)/shard_map/while
  186.3 3.1 copy-start.18
  198.7 18.2 %copy-start.1 = (bf16[1,256,768]{2,1,0:T(8,128)(2,1)S(1)}, bf16[1,256,768]{2,1,0:T(8,128)(2,1)}, u32[]{:S(2)}) copy-start(bf16[1,256,768]{2,1,0:T(8,128)(2,1)} %param.20) | copy-start | bytes 1179652
  201.2 11.0 %all-to-all-start.1 = ((bf16[4,2,24576]{2,1,0:T(2,128)(2,1)}), bf16[4,2,24576]{2,1,0:T(2,128)(2,1)S(1)}, u32[]{:S(2)}, u32[]{:S(2)}) async-start(bf16[4,2,24576]{2,1,0:T(2,128)(2,1)} %reshape.932), calls=%async_computation.1 | async-start | bytes 786432 | tf_op jit(solution)/shard_map/all_to_all | solution.py:438
  216.9 6.4 %slice-start = ((s8[4718592]{0:T(1024)(128)(4,1)}), s8[4194304]{0:T(1024)(128)(4,1)S(1)}, s32[]{:S(2)}) async-start(s8[4718592]{0:T(1024)(128)(4,1)} %bitcast.438), calls=%async_computation.4 | async-start | bytes 8388608
  219.0 11.9 %copy-start.3 = (f32[1,256,768]{2,1,0:T(8,128)}, f32[1,256,768]{2,1,0:T(8,128)S(1)}, u32[]{:S(2)}) copy-start(f32[1,256,768]{2,1,0:T(8,128)S(1)} %get-tuple-element.711) | copy-start | bytes 2359300
  219.0 11.9 %copy-start.52 = (f32[256]{0:T(256)}, f32[256]{0:T(256)S(1)}, u32[]{:S(2)}) copy-start(f32[256]{0:T(256)S(1)} %broadcast_multiply_fusion.4) | copy-start | bytes 3076
  219.3 11.6 %copy-start.59 = (f32[256]{0:T(256)}, f32[256]{0:T(256)S(1)}, u32[]{:S(2)}) copy-start(f32[256]{0:T(256)S(1)} %add_rsqrt_fusion) | copy-start | bytes 3076
  219.3 4.0 copy-start.67
  219.3 4.0 copy-start.69
  219.3 4.0 slice-start.1
  219.3 4.0 copy-start.73
  219.4 8.6 %slice-start.2 = ((s8[4718592]{0:T(1024)(128)(4,1)}), s8[524288]{0:T(1024)(128)(4,1)S(1)}, s32[]{:S(2)}) async-start(s8[4718592]{0:T(1024)(128)(4,1)} %bitcast.443), calls=%async_computation.6 | async-start | bytes 1048576
  223.3 7.6 %copy-start.75 = (f32[256,3072]{1,0:T(8,128)}, f32[256,3072]{1,0:T(8,128)S(1)}, u32[]{:S(2)}) copy-start(f32[256,3072]{1,0:T(8,128)S(1)} %convolution_add_fusion) | copy-start | bytes 9437188
  223.4 4.6 slice-start.3
  230.9 4.7 copy-start.7
  230.9 4.6 copy-start.34
  236.0 37.0 %copy-start.12 = (f32[1,1024,3,64]{1,3,2,0:T(8,128)S(1)}, f32[1,1024,3,64]{1,3,2,0:T(8,128)}, u32[]{:S(2)}) copy-start(f32[1,1024,3,64]{1,3,2,0:T(8,128)} %copy-done.11) | copy-start | bytes 2359300
  237.0 20.0 %all-to-all-start.2 = ((bf16[1,256,4,192]{1,3,0,2:T(8,128)(2,1)}), bf16[1,256,4,192]{1,3,0,2:T(8,128)(2,1)S(1)}, u32[]{:S(2)}, u32[]{:S(2)}) async-start(bf16[1,256,4,192]{1,3,0,2:T(8,128)(2,1)} %bitcast.405), calls=%async_computation.2 | async-start | bytes 786432 | tf_op jit(solution)/shard_map/all_to_all | solution.py:488
  241.2 4.5 copy-start.38
  241.2 31.8 %copy-start.19 = (f32[1,3,1024]{2,1,0:T(4,128)S(1)}, f32[1,3,1024]{2,1,0:T(4,128)}, u32[]{:S(2)}) copy-start(f32[1,3,1024]{2,1,0:T(4,128)} %get-tuple-element.492) | copy-start | bytes 36868
  274.2 4.9 copy-start.36
  280.3 6.4 %copy-start.21 = (f32[1,2048,3]{1,2,0:T(4,128)S(1)}, f32[1,2048,3]{1,2,0:T(4,128)}, u32[]{:S(2)}) copy-start(f32[1,2048,3]{1,2,0:T(4,128)} %get-tuple-element.1025) | copy-start | bytes 73732 | tf_op jit(solution)/shard_map/while
  280.3 6.4 %copy-start.22 = (f32[1,2048,3]{1,2,0:T(4,128)S(1)}, f32[1,2048,3]{1,2,0:T(4,128)}, u32[]{:S(2)}) copy-start(f32[1,2048,3]{1,2,0:T(4,128)} %get-tuple-element.1028) | copy-start | bytes 73732 | tf_op jit(solution)/shard_map/while
  280.3 8.2 %copy-start.14 = (bf16[1,1024,3,64]{1,3,2,0:T(8,128)(2,1)S(1)}, bf16[1,1024,3,64]{1,3,2,0:T(8,128)(2,1)}, u32[]{:S(2)}) copy-start(bf16[1,1024,3,64]{1,3,2,0:T(8,128)(2,1)} %get-tuple-element.1027) | copy-start | bytes 1179652 | tf_op jit(solution)/shard_map/while
  306.5 6.4 %copy-start.21 = (f32[1,2048,3]{1,2,0:T(4,128)S(1)}, f32[1,2048,3]{1,2,0:T(4,128)}, u32[]{:S(2)}) copy-start(f32[1,2048,3]{1,2,0:T(4,128)} %get-tuple-element.1025) | copy-start | bytes 73732 | tf_op jit(solution)/shard_map/while
  306.5 6.4 %copy-start.22 = (f32[1,2048,3]{1,2,0:T(4,128)S(1)}, f32[1,2048,3]{1,2,0:T(4,128)}, u32[]{:S(2)}) copy-start(f32[1,2048,3]{1,2,0:T(4,128)} %get-tuple-element.1028) | copy-start | bytes 73732 | tf_op jit(solution)/shard_map/while
  306.5 8.2 %copy-start.14 = (bf16[1,1024,3,64]{1,3,2,0:T(8,128)(2,1)S(1)}, bf16[1,1024,3,64]{1,3,2,0:T(8,128)(2,1)}, u32[]{:S(2)}) copy-start(bf16[1,1024,3,64]{1,3,2,0:T(8,128)(2,1)} %get-tuple-element.1027) | copy-start | bytes 1179652 | tf_op jit(solution)/shard_map/while
  334.6 7.6 %copy-start.37 = (f32[1,3,1024]{2,1,0:T(4,128)S(1)}, f32[1,3,1024]{2,1,0:T(4,128)}, u32[]{:S(2)}) copy-start(f32[1,3,1024]{2,1,0:T(4,128)} %get-tuple-element.1069) | copy-start | bytes 36868 | tf_op jit(solution)/shard_map/while
  352.4 7.6 %copy-start.37 = (f32[1,3,1024]{2,1,0:T(4,128)S(1)}, f32[1,3,1024]{2,1,0:T(4,128)}, u32[]{:S(2)}) copy-start(f32[1,3,1024]{2,1,0:T(4,128)} %get-tuple-element.1069) | copy-start | bytes 36868 | tf_op jit(solution)/shard_map/while
  371.8 6.4 %copy-start.10 = (bf16[1,256,4,1,192]{1,4,2,3,0:T(8,128)(2,1)S(1)}, bf16[1,256,4,1,192]{1,4,2,3,0:T(8,128)(2,1)}, u32[]{:S(2)}) copy-start(bf16[1,256,4,1,192]{1,4,2,3,0:T(8,128)(2,1)} %copy-done.9) | copy-start | bytes 1179652
  371.8 6.4 %copy-start.35 = (f32[768]{0:T(1024)S(1)}, f32[768]{0:T(1024)}, u32[]{:S(2)}) copy-start(f32[768]{0:T(1024)} %get-tuple-element.649) | copy-start | bytes 9220
  374.3 6.5 %copy-start.61 = (f32[768]{0:T(1024)S(1)}, f32[768]{0:T(1024)}, u32[]{:S(2)}) copy-start(f32[768]{0:T(1024)} %get-tuple-element.632) | copy-start | bytes 9220
  374.3 6.6 %copy-start.50 = (f32[3072]{0:T(1024)S(1)}, f32[3072]{0:T(1024)}, u32[]{:S(2)}) copy-start(f32[3072]{0:T(1024)} %get-tuple-element.755) | copy-start | bytes 36868
  374.3 6.7 %copy-start.62 = (f32[768]{0:T(1024)S(1)}, f32[768]{0:T(1024)}, u32[]{:S(2)}) copy-start(f32[768]{0:T(1024)} %get-tuple-element.642) | copy-start | bytes 9220
  374.3 6.8 %copy-start.4 = (f32[1,256,768]{2,1,0:T(8,128)S(1)}, f32[1,256,768]{2,1,0:T(8,128)}, u32[]{:S(2)}) copy-start(f32[1,256,768]{2,1,0:T(8,128)} %copy-done.3) | copy-start | bytes 2359300
  374.3 6.8 %copy-start.40 = (f32[768]{0:T(1024)S(1)}, f32[768]{0:T(1024)}, u32[]{:S(2)}) copy-start(f32[768]{0:T(1024)} %mul.555) | copy-start | bytes 9220
  374.3 6.8 %copy-start.42 = (f32[768]{0:T(1024)S(1)}, f32[768]{0:T(1024)}, u32[]{:S(2)}) copy-start(f32[768]{0:T(1024)} %get-tuple-element.646) | copy-start | bytes 9220
  374.4 6.8 %copy-start.47 = (f32[768]{0:T(1024)S(1)}, f32[768]{0:T(1024)}, u32[]{:S(2)}) copy-start(f32[768]{0:T(1024)} %get-tuple-element.645) | copy-start | bytes 9220
  374.4 6.8 %copy-start.53 = (f32[256]{0:T(256)S(1)}, f32[256]{0:T(256)}, u32[]{:S(2)}) copy-start(f32[256]{0:T(256)} %copy-done.52) | copy-start | bytes 3076
  374.4 6.8 %copy-start.60 = (f32[256]{0:T(256)S(1)}, f32[256]{0:T(256)}, u32[]{:S(2)}) copy-start(f32[256]{0:T(256)} %copy-done.59) | copy-start | bytes 3076
  374.4 29.4 %all-to-all-start.3 = ((bf16[1,1024,3,1,192]{4,2,3,0,1:T(4,128)(2,1)}), bf16[1,1024,3,1,192]{4,2,3,0,1:T(4,128)(2,1)S(1)}, u32[]{:S(2)}, u32[]{:S(2)}) async-start(bf16[1,1024,3,1,192]{4,2,3,0,1:T(4,128)(2,1)} %copy.100), calls=%async_computation.3 | async-start | bytes 4194304 | tf_op jit(solution)/shard_map/all_to_all | solution.py:546
  381.2 5.3 %copy-start.68 = (f32[768]{0:T(1024)S(1)}, f32[768]{0:T(1024)}, u32[]{:S(2)}) copy-start(f32[768]{0:T(1024)} %get-tuple-element.644) | copy-start | bytes 9220
  381.2 5.3 %copy-start.70 = (f32[256]{0:T(256)S(1)}, f32[256]{0:T(256)}, u32[]{:S(2)}) copy-start(f32[256]{0:T(256)} %compare_convert_fusion) | copy-start | bytes 3076
  381.2 5.3 %copy-start.74 = (bf16[1,256,768]{2,1,0:T(8,128)(2,1)S(1)}, bf16[1,256,768]{2,1,0:T(8,128)(2,1)}, u32[]{:S(2)}) copy-start(bf16[1,256,768]{2,1,0:T(8,128)(2,1)} %param.33) | copy-start | bytes 1179652
  381.2 5.3 %copy-start.76 = (f32[256,3072]{1,0:T(8,128)S(1)}, f32[256,3072]{1,0:T(8,128)}, u32[]{:S(2)}) copy-start(f32[256,3072]{1,0:T(8,128)} %copy-done.75) | copy-start | bytes 9437188
  415.5 98.3 %copy-start.57 = (bf16[4,1,128]{2,1,0:T(2,128)(2,1)S(1)}, bf16[4,1,128]{2,1,0:T(2,128)(2,1)}, u32[]{:S(2)}) copy-start(bf16[4,1,128]{2,1,0:T(2,128)(2,1)} %copy-done.56) | copy-start | bytes 3076
  415.5 99.7 %copy-start.6 = (f32[1,256,768]{2,1,0:T(8,128)S(1)}, f32[1,256,768]{2,1,0:T(8,128)}, u32[]{:S(2)}) copy-start(f32[1,256,768]{2,1,0:T(8,128)} %copy-done.5) | copy-start | bytes 2359300
  509.0 9.1 %copy-start.29 = (f32[24,768]{1,0:T(8,128)S(1)}, f32[24,768]{1,0:T(8,128)}, u32[]{:S(2)}) copy-start(f32[24,768]{1,0:T(8,128)} %get-tuple-element.503) | copy-start | bytes 221188
  509.0 9.7 %copy-start.28 = (f32[96,768]{1,0:T(8,128)S(1)}, f32[96,768]{1,0:T(8,128)}, u32[]{:S(2)}) copy-start(f32[96,768]{1,0:T(8,128)} %get-tuple-element.504) | copy-start | bytes 884740
  509.0 10.4 %copy-start.27 = (f32[24,3072]{1,0:T(8,128)S(1)}, f32[24,3072]{1,0:T(8,128)}, u32[]{:S(2)}) copy-start(f32[24,3072]{1,0:T(8,128)} %get-tuple-element.505) | copy-start | bytes 884740
  (29 other events, 46.8 us)

commit v2 on v0

v2 whole, which is shorter than its diff:
```python
from functools import partial
import math

import jax
import jax.numpy as jnp
from jax import lax
from jax.experimental import pallas as pl
from jax.experimental.pallas import tpu as pltpu
from jax.sharding import PartitionSpec as P

HEADS = 12
HEAD_DIM = 64
EPSILON = 1e-05
NEG_LARGE = -1e30
HIGHEST = lax.Precision.HIGHEST
F32 = jnp.float32
BF16 = jnp.bfloat16
AXES = ("dp", "blk", "head")
MESH_ID = pl.DeviceIdType.MESH
SCORE_SCALE = HEAD_DIM ** (-0.5)
EXP2_SCALE = SCORE_SCALE * math.log2(math.e)
VMEM_LIMIT = 60 * 2**20


def log2_of(count):
    assert count & (count - 1) == 0
    return count.bit_length() - 1


class Topo:
    def __init__(self, mesh):
        self.nd, self.nb, self.nh = (mesh.shape[axis] for axis in AXES)
        self.n = self.nd * self.nb * self.nh
        head_bits, blk_bits, dp_bits = (log2_of(size) for size in (self.nh, self.nb, self.nd))
        head = list(range(head_bits))
        blk = list(range(head_bits, head_bits + blk_bits))
        dp = list(range(head_bits + blk_bits, head_bits + blk_bits + dp_bits))
        self.orders = (dp + blk + head[1:] + head[:1], dp + head[1:] + blk + head[:1])
        self.phases = len(dp) + len(blk) + len(head)
        self.row = self.nb * self.nh
        self.groups = math.gcd(HEADS, self.row)
        self.split = self.row // self.groups

    def here(self):
        return (
            lax.axis_index("dp") * self.nb + lax.axis_index("blk")
        ) * self.nh + lax.axis_index("head")

    def coords(self, number):
        return (number // self.row, (number // self.nh) % self.nb, number % self.nh)

    def deltas(self, me, colour):
        steps = []
        for even, odd in zip(*self.orders):
            step = (1 - 2 * ((me // 2**even) % 2)) * 2**even
            if even != odd:
                other = (1 - 2 * ((me // 2**odd) % 2)) * 2**odd
                step = step + colour * (other - step)
            steps.append(step)
        return steps

    def plan(self):
        me = self.here()
        mine, other = self.deltas(me, me % 2), self.deltas(me, 1 - me % 2)

        def block(index):
            number = me
            use = other if index >> (self.phases - 1) & 1 else mine
            for bit in range(self.phases):
                if index >> bit & 1:
                    number = number + use[bit]
            return number

        return me, block, [self.coords(me + step) for step in mine]


def greet(devices):
    barrier = pltpu.get_barrier_semaphore()
    for device in devices:
        pl.semaphore_signal(barrier, 1, device_id=device, device_id_type=MESH_ID)
    pl.semaphore_wait(barrier, len(devices))


def remote(source, target, send, recv, device):
    return pltpu.make_async_remote_copy(
        src_ref=source,
        dst_ref=target,
        send_sem=send,
        recv_sem=recv,
        device_id=device,
        device_id_type=MESH_ID,
    )


def gather_steps(topo, ins, outs, send, recv, local):
    me, block, partner = topo.plan()
    phases = topo.phases
    sends = []

    def copy(k, index, phase):
        where = outs[k].at[block(index)]
        arrival = index + 2**phase
        return remote(
            ins[k] if index == 0 else where,
            where,
            send.at[k, arrival],
            recv.at[k, arrival],
            partner[phase],
        )

    def begin(k, index, phase):
        made = copy(k, index, phase)
        made.start()
        sends.append(made)

    for k in range(len(ins)):
        for phase in range(phases):
            begin(k, 0, phase)
    own = [pltpu.make_async_copy(ins[k], outs[k].at[me], local.at[k]) for k in range(len(ins))]
    for made in own:
        made.start()
    yield
    for index in range(1, 2**phases):
        top = index.bit_length() - 1
        where = block(index)
        for k in range(len(ins)):
            remote(
                outs[k].at[where],
                outs[k].at[where],
                send.at[k, index],
                recv.at[k, index],
                partner[top],
            ).wait_recv()
            for phase in range(top + 1, phases):
                begin(k, index, phase)
        yield
    for made in sends:
        made.wait_send()
    for made in own:
        made.wait()


def reduce_steps(topo, ins, outs, arrived, send, recv):
    me, block, partner = topo.plan()
    phases = topo.phases
    half = 2 ** (phases - 1)
    sends = []

    def copy(k, index, source):
        return remote(
            source,
            arrived[k].at[index],
            send.at[k, index],
            recv.at[k, index],
            partner[index.bit_length() - 1],
        )

    def begin(k, index, source):
        made = copy(k, index, source)
        made.start()
        sends.append(made)

    for index in range(2 * half - 1, half - 1, -1):
        for k in range(len(ins)):
            begin(k, index, ins[k].at[block(index)])
    yield
    for index in range(half - 1, -1, -1):
        top = index.bit_length() - 1
        where = block(index)
        for k in range(len(ins)):
            total = ins[k][where].astype(F32)
            for phase in range(phases - 1, top, -1):
                slot = arrived[k].at[2**phase + index]
                copy(k, 2**phase + index, slot).wait_recv()
                total = total + slot[...].astype(F32)
            if index == 0:
                outs[k][...] = total
            else:
                slot = arrived[k].at[half + index]
                slot[...] = total.astype(slot.dtype)
                begin(k, index, slot)
        yield
    for made in sends:
        made.wait_send()


def finish(steps):
    for _ in steps:
        pass


def gather_kernel(topo, count, *refs):
    ins, outs = refs[:count], refs[count : 2 * count]
    greet(topo.plan()[2])
    finish(gather_steps(topo, ins, outs, *refs[2 * count :]))


def comm_params(collective_id):
    return pltpu.CompilerParams(
        collective_id=collective_id, has_side_effects=True, vmem_limit_bytes=VMEM_LIMIT
    )


def dma(*shape):
    return pltpu.SemaphoreType.DMA(shape)


def in_vmem(count):
    return [pl.BlockSpec(memory_space=pltpu.VMEM)] * count


def in_any(count):
    return [pl.BlockSpec(memory_space=pl.ANY)] * count


def gathered_shapes(topo, arrays):
    return [jax.ShapeDtypeStruct((topo.n,) + a.shape, a.dtype) for a in arrays]


def gather_sems(topo, count):
    return [dma(count, topo.n), dma(count, topo.n), dma(count)]


def gather(topo, arrays, collective_id):
    count = len(arrays)
    return pl.pallas_call(
        partial(gather_kernel, topo, count),
        out_shape=gathered_shapes(topo, arrays),
        in_specs=in_vmem(count),
        out_specs=in_any(count),
        scratch_shapes=gather_sems(topo, count),
        compiler_params=comm_params(collective_id),
        name="gather",
    )(*arrays)


def reduce_kernel(topo, count, *refs):
    ins, outs, arrived = refs[:count], refs[count : 2 * count], refs[2 * count : 3 * count]
    greet(topo.plan()[2])
    finish(reduce_steps(topo, ins, outs, arrived, *refs[3 * count :]))


def owned_shapes(arrays):
    return [jax.ShapeDtypeStruct(a.shape[1:], F32) for a in arrays]


def arrival_scratch(arrays):
    return [pltpu.VMEM(a.shape, a.dtype) for a in arrays]


def reduce_sems(topo, count):
    return [dma(count, topo.n), dma(count, topo.n)]


def reduce_scatter(topo, arrays, collective_id):
    count = len(arrays)
    return pl.pallas_call(
        partial(reduce_kernel, topo, count),
        out_shape=owned_shapes(arrays),
        in_specs=in_vmem(count),
        out_specs=in_vmem(count),
        scratch_shapes=arrival_scratch(arrays) + reduce_sems(topo, count),
        compiler_params=comm_params(collective_id),
        name="reduce",
    )(*arrays)


def dot(left, right):
    return lax.dot_general(left, right, (((1,), (0,)), ((), ())), preferred_element_type=F32)


def repeat(count, step, state, tick):
    if count <= 8:
        for index in range(count):
            state = step(index, state)
            tick()
        return state
    return lax.fori_loop(0, count, step, state)


def span(index, size):
    if isinstance(index, int):
        return slice(index * size, (index + 1) * size)
    return pl.ds(pl.multiple_of(index * size, size), size)


def fit(total, most):
    return math.gcd(total, most)


def keys_with_mask(key_t, length):
    slots = key_t.shape[1]
    slot = lax.broadcasted_iota(jnp.int32, (slots, HEAD_DIM), 0)
    lane = lax.broadcasted_iota(jnp.int32, (slots, HEAD_DIM), 1)
    mask = jnp.where((lane == 0) & (slot >= length), NEG_LARGE, 0.0).astype(BF16)
    return jnp.concatenate([key_t.T, mask], axis=1)


def queries_with_one(query_t):
    row = lax.broadcasted_iota(jnp.int32, query_t.shape, 0)
    return jnp.concatenate([query_t, jnp.where(row == 0, 1.0, 0.0).astype(BF16)], axis=0)


def attend_head(head, length, qt, kt, vt, kn, scores, ot, low, lse, tick):
    slots, queries = kt.shape[1], qt.shape[1]
    width = scores.shape[1]
    step_keys = fit(slots, 256)
    rows = slice(head * HEAD_DIM, (head + 1) * HEAD_DIM)
    kn[...] = keys_with_mask(kt[rows, :], length)

    def one_width(index, _):
        columns = span(index, width)
        query = queries_with_one(qt[rows, columns])

        def find_peak(step, peak):
            keys = span(step, step_keys)
            part = dot(kn[keys, :], query)
            scores[keys, :] = part
            return jnp.maximum(peak, jnp.max(part, axis=0, keepdims=True))

        count = slots // step_keys
        peak = repeat(count, find_peak, jnp.full((1, width), NEG_LARGE, F32), tick)
        peak = peak * EXP2_SCALE

        def add_values(step, state):
            total, summed = state
            keys = span(step, step_keys)
            weights = jnp.exp2(scores[keys, :] * EXP2_SCALE - peak)
            total = total + jnp.sum(weights, axis=0, keepdims=True)
            return (total, summed + dot(vt[rows, keys], weights.astype(BF16)))

        start = (jnp.zeros((1, width), F32), jnp.zeros((HEAD_DIM, width), F32))
        total, summed = repeat(count, add_values, start, tick)
        output = summed / total
        ot[rows, columns] = output
        low[rows, columns] = output.astype(BF16)
        lse[head : head + 1, columns] = peak + jnp.log2(total)
        return 0

    if queries == width:
        one_width(0, 0)
    else:
        lax.fori_loop(0, queries // width, one_width, 0)


def attend_back_head(head, length, qt, kt, vt, gt, ot, lse, kn, vn, qn, gn, dq_sum, dq, dk, dv, tick):
    slots, queries = kt.shape[1], qt.shape[1]
    step_keys = fit(slots, 512)
    rows = slice(head * HEAD_DIM, (head + 1) * HEAD_DIM)
    kn[...] = keys_with_mask(kt[rows, :], length)
    vn[...] = vt[rows, :].T
    qn[...] = qt[rows, :].T
    gn[...] = gt[rows, :].T
    query = queries_with_one(qt[rows, :])
    grad = gt[rows, :]
    delta = jnp.sum(grad.astype(F32) * ot[rows, :], axis=0, keepdims=True)
    log_sum = lse[head : head + 1, :]
    dq_sum[...] = jnp.zeros_like(dq_sum)

    def one_step(step, _):
        keys = span(step, step_keys)
        weights = jnp.exp2(dot(kn[keys, :], query) * EXP2_SCALE - log_sum)
        grad_weights = dot(vn[keys, :], grad)
        grad_scores = (weights * (grad_weights - delta)).astype(BF16)
        dv[rows, keys] = dot(weights.astype(BF16), gn[...]).T.astype(BF16)
        dk[rows, keys] = (dot(grad_scores, qn[...]).T * SCORE_SCALE).astype(BF16)
        dq_sum[...] += dot(kt[rows, keys], grad_scores)
        return 0

    repeat(slots // step_keys, one_step, 0, tick)
    dq[rows, :] = (dq_sum[...] * SCORE_SCALE).astype(BF16)


class RowPlan:
    def __init__(self, topo):
        self.topo = topo
        self.groups, self.split = topo.groups, topo.split
        self.place = topo.here() % topo.row
        self.group, self.member = self.place // topo.split, self.place % topo.split

    def device(self, group, member):
        place = group * self.split + member
        topo = self.topo
        return (lax.axis_index("dp"), place // topo.nh, place % topo.nh)

    def across(self):
        return [(self.group + step) % self.groups for step in range(1, self.groups)]

    def beside(self):
        return [(self.member + step) % self.split for step in range(1, self.split)]

    def partners(self):
        return [self.device(group, self.member) for group in self.across()] + [
            self.device(self.group, member) for member in self.beside()
        ]


def columns_at(index, size):
    return pl.ds(pl.multiple_of(index * size, size), size)


def attend_kernel(topo, count, length_ref, qkv, *refs):
    shards, refs = refs[:count], refs[count:]
    attended, qt, kt, vt, ot, lse = refs[:6]
    outs, refs = refs[6 : 6 + count], refs[6 + count :]
    low, kn, scores, q_send, q_recv, kv_send, kv_recv, pass_send, back_send, back_recv, local = refs[:11]
    plan = RowPlan(topo)
    tokens = qkv.shape[3]
    greet(plan.partners() + topo.plan()[2])
    sends = []

    def begin(made):
        made.start()
        sends.append(made)

    own = plan.group * plan.split + plan.member
    full = (kt, vt)

    def slot_of(group, member):
        return columns_at(group * plan.split + member, tokens)

    for step, group in enumerate(plan.across()):
        device = plan.device(group, plan.member)
        for which in range(2):
            begin(
                remote(
                    qkv.at[1 + which, group],
                    full[which].at[:, slot_of(plan.group, plan.member)],
                    kv_send.at[which, step],
                    kv_recv.at[which, own],
                    device,
                )
            )
    for step, group in enumerate(plan.across()):
        begin(
            remote(
                qkv.at[0, group],
                qt.at[:, columns_at(plan.group, tokens)],
                q_send.at[step],
                q_recv.at[plan.group],
                plan.device(group, plan.member),
            )
        )
    mine = [
        pltpu.make_async_copy(
            qkv.at[0, plan.group], qt.at[:, columns_at(plan.group, tokens)], local.at[0]
        )
    ]
    for which in range(2):
        mine.append(
            pltpu.make_async_copy(
                qkv.at[1 + which, plan.group],
                full[which].at[:, slot_of(plan.group, plan.member)],
                local.at[1 + which],
            )
        )
    for made in mine:
        made.start()

    def hand_on(which, step, group, source):
        for index, member in enumerate(plan.beside()):
            begin(
                remote(
                    source,
                    full[which].at[:, slot_of(group, plan.member)],
                    pass_send.at[which, step, index],
                    kv_recv.at[which, group * plan.split + plan.member],
                    plan.device(plan.group, member),
                )
            )

    def wait_keys(which, group, member):
        where = full[which].at[:, slot_of(group, member)]
        remote(
            where,
            where,
            kv_send.at[which, 0],
            kv_recv.at[which, group * plan.split + member],
            plan.device(group, plan.member),
        ).wait_recv()

    for which in range(2):
        hand_on(which, 0, plan.group, qkv.at[1 + which, plan.group])
    weights = gather_steps(topo, shards, outs, *refs[11:])
    next(weights)

    def tick():
        next(weights, None)

    for step, group in enumerate(plan.across()):
        for which in range(2):
            wait_keys(which, group, plan.member)
            hand_on(
                which, step + 1, group, full[which].at[:, slot_of(group, plan.member)]
            )
        tick()
    for member in plan.beside():
        for group in [plan.group] + plan.across():
            for which in range(2):
                wait_keys(which, group, member)
    for step, group in enumerate(plan.across()):
        where = qt.at[:, columns_at(group, tokens)]
        remote(
            where, where, q_send.at[step], q_recv.at[group], plan.device(group, plan.member)
        ).wait_recv()
    for made in mine:
        made.wait()

    heads = qt.shape[0] // HEAD_DIM
    lse[...] = jnp.zeros_like(lse)
    returned = []
    for head in range(heads):
        attend_head(head, length_ref[0], qt, kt, vt, kn, scores, ot, low, lse, tick)
        rows = pl.ds(head * HEAD_DIM, HEAD_DIM)
        for step, group in enumerate(plan.across()):
            begin(
                remote(
                    low.at[rows, columns_at(group, tokens)],
                    attended.at[plan.group, rows],
                    back_send.at[head, step],
                    back_recv.at[head, plan.group],
                    plan.device(group, plan.member),
                )
            )
    made = pltpu.make_async_copy(
        low.at[:, columns_at(plan.group, tokens)], attended.at[plan.group], local.at[0]
    )
    made.start()
    finish(weights)
    made.wait()
    for head in range(heads):
        rows = pl.ds(head * HEAD_DIM, HEAD_DIM)
        for step, group in enumerate(plan.across()):
            where = attended.at[group, rows]
            remote(
                where,
                where,
                back_send.at[head, step],
                back_recv.at[head, group],
                plan.device(group, plan.member),
            ).wait_recv()
    for made in sends:
        made.wait_send()


def attend(topo, lengths, qkv, shards, slots, collective_id):
    count = len(shards)
    groups, split = topo.groups, topo.split
    width, tokens = qkv.shape[2:]
    heads = width // HEAD_DIM
    queries = groups * tokens
    score_width = fit(queries, max(128, 2**21 // slots))
    shapes = [
        jax.ShapeDtypeStruct((groups, width, tokens), BF16),
        jax.ShapeDtypeStruct((width, queries), BF16),
        jax.ShapeDtypeStruct((width, slots), BF16),
        jax.ShapeDtypeStruct((width, slots), BF16),
        jax.ShapeDtypeStruct((width, queries), F32),
        jax.ShapeDtypeStruct((8, queries), F32),
    ]
    results = pl.pallas_call(
        partial(attend_kernel, topo, count),
        out_shape=shapes + gathered_shapes(topo, shards),
        in_specs=[pl.BlockSpec(memory_space=pltpu.SMEM)] + in_vmem(1 + count),
        out_specs=in_vmem(len(shapes)) + in_any(count),
        scratch_shapes=[
            pltpu.VMEM((width, queries), BF16),
            pltpu.VMEM((slots, 2 * HEAD_DIM), BF16),
            pltpu.VMEM((slots, score_width), F32),
            dma(groups),
            dma(groups),
            dma(2, groups),
            dma(2, groups * split),
            dma(2, groups, split),
            dma(heads, groups),
            dma(heads, groups),
            dma(3),
        ]
        + gather_sems(topo, count),
        compiler_params=comm_params(collective_id),
        name="attend",
    )(lengths, qkv, *shards)
    return results[: len(shapes)], results[len(shapes) :]


def attend_back_kernel(topo, count, length_ref, grad, qt, kt, vt, ot, lse, *refs):
    terms, refs = refs[:count], refs[count:]
    back, owned, refs = refs[0], refs[1 : 1 + count], refs[1 + count :]
    gt, dq, dk, dv, partial_sums, kn, vn, qn, gn, dq_sum, refs = *refs[:10], refs[10:]
    g_send, g_recv, part_send, part_recv, back_send, back_recv, local = refs[:7]
    arrived, refs = refs[7 : 7 + count], refs[7 + count :]
    plan = RowPlan(topo)
    tokens = grad.shape[2]
    greet(plan.partners() + (topo.plan()[2] if count else []))
    sends = []

    def begin(made):
        made.start()
        sends.append(made)

    for step, group in enumerate(plan.across()):
        begin(
            remote(
                grad.at[group],
                gt.at[:, columns_at(plan.group, tokens)],
                g_send.at[step],
                g_recv.at[plan.group],
                plan.device(group, plan.member),
            )
        )
    mine = pltpu.make_async_copy(
        grad.at[plan.group], gt.at[:, columns_at(plan.group, tokens)], local.at[0]
    )
    mine.start()
    sums = reduce_steps(topo, terms, owned, arrived, *refs) if count else iter(())
    next(sums, None)

    def tick():
        next(sums, None)

    for step, group in enumerate(plan.across()):
        where = gt.at[:, columns_at(group, tokens)]
        remote(
            where, where, g_send.at[step], g_recv.at[group], plan.device(group, plan.member)
        ).wait_recv()
    mine.wait()
    heads = qt.shape[0] // HEAD_DIM
    pairs = (dk, dv)

    def slot_of(group, member):
        return columns_at(group * plan.split + member, tokens)

    for head in range(heads):
        attend_back_head(
            head, length_ref[0], qt, kt, vt, gt, ot, lse, kn, vn, qn, gn, dq_sum, dq, dk, dv, tick
        )
        rows = pl.ds(head * HEAD_DIM, HEAD_DIM)
        for index, member in enumerate(plan.beside()):
            for group in range(plan.groups):
                for which in range(2):
                    begin(
                        remote(
                            pairs[which].at[rows, slot_of(group, member)],
                            partial_sums.at[plan.split - 2 - index, which, group, rows],
                            part_send.at[head, which, group, index],
                            part_recv.at[head, which, group, plan.split - 2 - index],
                            plan.device(plan.group, member),
                        )
                    )
        for step, group in enumerate(plan.across()):
            begin(
                remote(
                    dq.at[rows, columns_at(group, tokens)],
                    back.at[0, plan.group, rows],
                    back_send.at[head, 0, step],
                    back_recv.at[head, 0, plan.group],
                    plan.device(group, plan.member),
                )
            )
    for head in range(heads):
        rows = pl.ds(head * HEAD_DIM, HEAD_DIM)
        for step, group in enumerate(plan.across() + [plan.group]):
            for which in range(2):
                where = pairs[which].at[rows, slot_of(group, plan.member)]
                total = where[...].astype(F32)
                for index, member in enumerate(plan.beside()):
                    slot = partial_sums.at[index, which, group, rows]
                    remote(
                        slot,
                        slot,
                        part_send.at[head, which, group, index],
                        part_recv.at[head, which, group, index],
                        plan.device(plan.group, member),
                    ).wait_recv()
                    total = total + slot[...].astype(F32)
                where[...] = total.astype(BF16)
                if step < plan.groups - 1:
                    begin(
                        remote(
                            where,
                            back.at[1 + which, plan.group, rows],
                            back_send.at[head, 1 + which, step],
                            back_recv.at[head, 1 + which, plan.group],
                            plan.device(group, plan.member),
                        )
                    )
            tick()
    back[0, plan.group] = dq[:, columns_at(plan.group, tokens)]
    for which in range(2):
        back[1 + which, plan.group] = pairs[which][:, slot_of(plan.group, plan.member)]
    finish(sums)
    for head in range(heads):
        rows = pl.ds(head * HEAD_DIM, HEAD_DIM)
        for which in range(3):
            for step, group in enumerate(plan.across()):
                where = back.at[which, group, rows]
                remote(
                    where,
                    where,
                    back_send.at[head, which, step],
                    back_recv.at[head, which, group],
                    plan.device(group, plan.member),
                ).wait_recv()
    for made in sends:
        made.wait_send()


def attend_back(topo, lengths, grad, saved, terms, collective_id):
    count = len(terms)
    groups, split = topo.groups, topo.split
    width, tokens = grad.shape[1:]
    heads = width // HEAD_DIM
    queries, slots = saved[0].shape[1], saved[1].shape[1]
    results = pl.pallas_call(
        partial(attend_back_kernel, topo, count),
        out_shape=[jax.ShapeDtypeStruct((3, groups, width, tokens), BF16)] + owned_shapes(terms),
        in_specs=[pl.BlockSpec(memory_space=pltpu.SMEM)] + in_vmem(1 + len(saved) + count),
        out_specs=in_vmem(1 + count),
        scratch_shapes=[
            pltpu.VMEM((width, queries), BF16),
            pltpu.VMEM((width, queries), BF16),
            pltpu.VMEM((width, slots), BF16),
            pltpu.VMEM((width, slots), BF16),
            pltpu.VMEM((max(split - 1, 1), 2, groups, width, tokens), BF16),
            pltpu.VMEM((slots, 2 * HEAD_DIM), BF16),
            pltpu.VMEM((slots, HEAD_DIM), BF16),
            pltpu.VMEM((queries, HEAD_DIM), BF16),
            pltpu.VMEM((queries, HEAD_DIM), BF16),
            pltpu.VMEM((HEAD_DIM, queries), F32),
            dma(groups),
            dma(groups),
            dma(heads, 2, groups, split),
            dma(heads, 2, groups, split),
            dma(heads, 3, groups),
            dma(heads, 3, groups),
            dma(1),
        ]
        + arrival_scratch(terms)
        + (reduce_sems(topo, count) if count else []),
        compiler_params=comm_params(collective_id),
        name="attend_back",
    )(lengths, grad, *saved, *terms)
    return results[0], results[1:]


def rotary_tables(positions):
    half_dim = HEAD_DIM // 2
    frequency = jnp.exp(
        jnp.arange(half_dim, dtype=F32) * (-2.0 * math.log(10000.0) / HEAD_DIM)
    )
    angles = frequency[:, None] * positions.astype(F32)[None, :]
    return (jnp.cos(angles), jnp.sin(angles))


def rotate(values, cosine, sine):
    first_half, second_half = jnp.split(values, 2, axis=1)
    return jnp.concatenate(
        [
            first_half * cosine - second_half * sine,
            second_half * cosine + first_half * sine,
        ],
        axis=1,
    )


def normalize(values):
    center = values - jnp.mean(values, axis=-1, keepdims=True)
    inverse = lax.rsqrt(jnp.mean(center * center, axis=-1, keepdims=True) + EPSILON)
    return (center * inverse, inverse)


def normalize_back(grad_unit, unit_values, inverse):
    mean_grad = jnp.mean(grad_unit, axis=-1, keepdims=True)
    mean_cross = jnp.mean(grad_unit * unit_values, axis=-1, keepdims=True)
    return (grad_unit - mean_grad - unit_values * mean_cross) * inverse


def product(equation, left, right):
    return jnp.einsum(equation, left, right, preferred_element_type=F32)


def joined(blocks):
    return blocks.reshape(-1, blocks.shape[-1])


def body(
    topo,
    tokens,
    cond,
    lengths,
    ada_weight,
    ada_bias,
    norm1_gain,
    qkv_weight,
    out_weight,
    norm2_gain,
    up_weight,
    up_bias,
    down_weight,
    down_bias,
    out_grad,
):
    devices = topo.n
    rows_all = topo.nd
    _, tok_count, width = tokens.shape
    slots = tok_count * topo.row
    cond_all = lax.all_gather(cond, "dp", axis=0, tiled=True)
    mod_columns = ada_weight.shape[1]
    mod_own = jnp.dot(cond_all, ada_weight, preferred_element_type=F32) + ada_bias.astype(F32)
    vectors = [norm1_gain, norm2_gain, up_bias, down_bias]
    small = jnp.concatenate([mod_own.reshape(-1)] + [v.astype(F32) for v in vectors])
    small = jnp.pad(small, (0, -small.shape[0] % 1024)).reshape(-1, 128)
    small_all, qkv_t = gather(topo, [small, qkv_weight.T], 0)
    qkv_t = joined(qkv_t)
    small_all = small_all.reshape(devices, -1)
    mod_all = small_all[:, : rows_all * mod_columns].reshape(devices, rows_all, mod_columns)
    modulation = lax.dynamic_index_in_dim(
        mod_all, lax.axis_index("dp"), 1, keepdims=False
    ).reshape(6, 1, width)
    shift_one, scale_one, gate_one, shift_two, scale_two, gate_two = modulation
    cut = rows_all * mod_columns
    full_vectors = []
    for v in vectors:
        full_vectors.append(small_all[:, cut : cut + v.shape[0]].reshape(-1))
        cut += v.shape[0]
    gain_one, gain_two, up_bias_full, down_bias_full = full_vectors
    seq_index = lax.axis_index("blk") * topo.nh + lax.axis_index("head")
    positions = seq_index * tok_count + jnp.arange(tok_count, dtype=jnp.int32)
    slot_live = (positions < lengths[0]).astype(F32)[:, None]
    cosine, sine = rotary_tables(positions)
    tokens_wide = tokens[0].astype(F32)
    unit_one, inverse_one = normalize(tokens_wide)
    normed_one = unit_one * gain_one
    hidden_one = (normed_one * (1.0 + scale_one) + shift_one).astype(BF16)
    projected = product("ed,td->et", qkv_t, hidden_one).reshape(
        3, HEADS, HEAD_DIM, tok_count
    )
    turned = jnp.stack(
        [rotate(projected[0], cosine, sine), rotate(projected[1], cosine, sine), projected[2]]
    ).astype(BF16)
    (attended, *saved), weights = attend(
        topo,
        lengths,
        turned.reshape(3, topo.groups, -1, tok_count),
        [out_weight.T, up_weight.T, down_weight.T, ada_weight.T],
        slots,
        1,
    )
    out_t, up_t, down_t, ada_t = (joined(w) for w in weights)
    attended = joined(attended)
    branch_one = product("dt,ed->te", attended, out_t)
    middle = tokens_wide + gate_one * branch_one
    unit_two, inverse_two = normalize(middle)
    normed_two = unit_two * gain_two
    hidden_two = (normed_two * (1.0 + scale_two) + shift_two).astype(BF16)
    inner = product("td,fd->tf", hidden_two, up_t) + up_bias_full
    activated, gelu_back = jax.vjp(partial(jax.nn.gelu, approximate=True), inner)
    activated = activated.astype(BF16)
    branch_two = product("tf,df->td", activated, down_t) + down_bias_full
    result = middle + gate_two * branch_two
    grad_out = out_grad[0].astype(F32) * slot_live
    grad_gate_two = jnp.sum(grad_out * branch_two, axis=0)
    grad_branch_two = (grad_out * gate_two).astype(BF16)
    grad_down = product("td,tf->df", grad_branch_two, activated)
    grad_down_bias = jnp.sum(grad_branch_two.astype(F32), axis=0)
    grad_activated = product("td,df->tf", grad_branch_two, down_t)
    grad_inner = gelu_back(grad_activated)[0].astype(BF16)
    grad_up = product("tf,td->fd", grad_inner, hidden_two)
    grad_up_bias = jnp.sum(grad_inner.astype(F32), axis=0)
    grad_hidden_two = product("tf,fd->td", grad_inner, up_t)
    grad_shift_two = jnp.sum(grad_hidden_two, axis=0)
    grad_scale_two = jnp.sum(grad_hidden_two * normed_two, axis=0)
    grad_normed_two = grad_hidden_two * (1.0 + scale_two)
    grad_gain_two = jnp.sum(grad_normed_two * unit_two, axis=0)
    grad_middle = grad_out + normalize_back(grad_normed_two * gain_two, unit_two, inverse_two)
    grad_gate_one = jnp.sum(grad_middle * branch_one, axis=0)
    grad_branch_one = (grad_middle * gate_one).astype(BF16)
    grad_out_proj = product("te,dt->ed", grad_branch_one, attended)
    grad_attended = product("ed,te->dt", out_t, grad_branch_one).astype(BF16)
    terms = [
        g.astype(BF16).reshape(devices, -1, g.shape[-1])
        for g in (grad_out_proj, grad_up, grad_down)
    ]
    fused = slots <= 4096
    grad_heads, owned = attend_back(
        topo,
        lengths,
        grad_attended.reshape(topo.groups, -1, tok_count),
        saved,
        terms if fused else [],
        2,
    )
    if not fused:
        owned = reduce_scatter(topo, terms, 3)
    out_own, up_own, down_own = owned
    grad_heads = grad_heads.reshape(3, HEADS, HEAD_DIM, tok_count)
    turned_back = [rotate(grad_heads[i].astype(F32), cosine, -sine) for i in range(2)]
    grad_projected = jnp.stack([turned_back[0], turned_back[1], grad_heads[2].astype(F32)])
    grad_projected = grad_projected.astype(BF16).reshape(-1, tok_count)
    grad_qkv = product("et,td->ed", grad_projected, hidden_one)
    grad_hidden_one = product("et,ed->td", grad_projected, qkv_t)
    grad_shift_one = jnp.sum(grad_hidden_one, axis=0)
    grad_scale_one = jnp.sum(grad_hidden_one * normed_one, axis=0)
    grad_normed_one = grad_hidden_one * (1.0 + scale_one)
    grad_gain_one = jnp.sum(grad_normed_one * unit_one, axis=0)
    grad_tokens = grad_middle + normalize_back(grad_normed_one * gain_one, unit_one, inverse_one)
    grad_modulation = jnp.concatenate(
        [
            grad_shift_one,
            grad_scale_one,
            grad_gate_one,
            grad_shift_two,
            grad_scale_two,
            grad_gate_two,
        ],
    )
    cond_part = jnp.dot(grad_modulation[None], ada_t.astype(F32), precision=HIGHEST)
    row_here = jnp.arange(rows_all, dtype=jnp.int32) == lax.axis_index("dp")
    plane = jnp.repeat(row_here, topo.row)
    mod_blocks = jnp.where(
        row_here[None, :, None], grad_modulation.reshape(devices, 1, mod_columns), 0.0
    )
    small_grads = jnp.concatenate(
        [mod_blocks.reshape(devices, -1)]
        + [
            v.reshape(devices, -1)
            for v in (grad_gain_one, grad_gain_two, grad_up_bias, grad_down_bias)
        ]
        + [jnp.where(plane[:, None], cond_part, 0.0)],
        axis=1,
    )
    small_grads = jnp.pad(small_grads, ((0, 0), (0, -small_grads.shape[1] % 1024)))
    small_own, qkv_own = reduce_scatter(
        topo,
        [
            small_grads.reshape(devices, -1, 128),
            grad_qkv.astype(BF16).reshape(devices, -1, grad_qkv.shape[-1]),
        ],
        4,
    )
    small_own = small_own.reshape(-1)
    cut = rows_all * mod_columns
    mod_grads = small_own[:cut].reshape(rows_all, mod_columns)
    vector_grads = []
    for v in vectors:
        vector_grads.append(small_own[cut : cut + v.shape[0]])
        cut += v.shape[0]
    grad_cond = small_own[cut : cut + cond.shape[1]].reshape(1, -1)
    grad_ada = jnp.dot(cond_all.astype(F32).T, mod_grads, precision=HIGHEST)
    return (
        result.astype(BF16)[None],
        grad_tokens[None],
        grad_cond,
        grad_ada,
        jnp.sum(mod_grads, axis=0),
        vector_grads[0],
        qkv_own.T,
        out_own.T,
        vector_grads[1],
        up_own.T,
        vector_grads[2],
        down_own.T,
        vector_grads[3],
    )


def solution(mesh):
    rows, owners = P("dp", ("blk", "head"), None), ("dp", "blk", "head")
    matrix, vector = P(None, owners), P(owners)
    params = [matrix, vector, vector, matrix, matrix, vector, matrix, vector, matrix, vector]
    return jax.shard_map(
        partial(body, Topo(mesh)),
        mesh=mesh,
        in_specs=(rows, P("dp", None), P("dp"), *params, rows),
        out_specs=(rows, rows, P("dp", None), *params),
        check_vma=False,
    )
```

time: 1110 us -> 318 us (0.29)
  waiting for transfers between devices: 672 us -> 0 us
  Pallas kernels: 0 us -> 219 us
  blocking collectives: 152 us -> 12.8 us
  matrix products: 150 us -> 46.1 us
  other arithmetic: 51.9 us -> 8.26 us
  local copies, waits for them, and re-layouts: 44.5 us -> 25.7 us
  starting transfers between devices: 15.2 us -> 0 us
  between operations: 16 us -> 1.94 us
    reduce_scatter x5 -> x0, waiting for transfers between devices: 499 us -> none  [the longest x1 142 us: body(): lax.psum_scatter(grad_up, ('dp', 'blk', 'head'), scatter_dimension=1, til...]
    pallas_call x0 -> x4, Pallas kernels: none -> 219 us  [the longest x1 82.3 us: attend(): pl.pallas_call(partial(attend_kernel, topo, count), out_shape=shapes + ga...]
    all_gather x5 -> x0, waiting for transfers between devices: 125 us -> none  [the longest x1 59.5 us: body(): lax.all_gather(qkv_weight, ('dp', 'blk', 'head'), axis=1, tiled=True)]
    dot_general x28 -> x15, matrix products: 150 us -> 46.1 us  [the longest x12 43.8 us: product(): return jnp.einsum(equation, left, right, preferred_element_type=F32)]
    unnamed x2 -> x0, blocking collectives: 82.3 us -> none
    all_to_all x4 -> x0, waiting for transfers between devices: 44.3 us -> none  [the longest x1 23.5 us: body(): lax.all_to_all(grad_stack.reshape(row_count, group_rows, 3, 1, local_widt...]
    all_gather x6 -> x1, blocking collectives: 56.6 us -> 12.8 us  [body(): cond_all = lax.all_gather(cond, 'dp', axis=0, tiled=True)]
    reduce_sum x5 -> x1, other arithmetic: 19.7 us -> 0.58 us  [body(): jnp.sum(mod_grads, axis=0)]
  transfers between devices with their start and end apart: 14 -> 0, of which waited for: 10 -> 0; matrix products, arithmetic and copies ran while one was open for 11% -> 0% of each run, Pallas kernels for 0% -> 0%
where the time goes in v2:
time: 318 us; the launch traced here: 314 us
  Pallas kernels  219 us (69%)
  matrix products  46.1 us (14%)
  local copies, waits for them, and re-layouts  25.7 us (8%)
  blocking collectives  12.8 us (4%)
  other arithmetic  8.26 us (3%)
    pallas_call x1, Pallas kernels, attend(): pl.pallas_call(partial(attend_kernel, topo, count), out_shape=shapes + ga...  82.3 us
    pallas_call x1, Pallas kernels, attend_back(): pl.pallas_call(partial(attend_back_kernel, topo, count), out_shape=[jax.S...  81.4 us
    dot_general x12, matrix products, product(): return jnp.einsum(equation, left, right, preferred_element_type=F32)  43.8 us
    pallas_call x1, Pallas kernels, reduce_scatter(): pl.pallas_call(partial(reduce_kernel, topo, count), out_shape=owned_shape...  30.1 us
    pallas_call x1, Pallas kernels, gather(): pl.pallas_call(partial(gather_kernel, topo, count), out_shape=gathered_sh...  25.3 us
    all_gather x1, blocking collectives, body(): cond_all = lax.all_gather(cond, 'dp', axis=0, tiled=True)  12.8 us
    unnamed x50, local copies, waits for them, and re-layouts  10.9 us

profile of v2, /device:TPU:0, one launch (start us, length us, event | category | flops | bytes accessed | tf_op | source)
XLA Modules:
  0.0 313.9 jit_solution(8222556550366856401)
XLA Ops:
  0.6 0.7 convert_element_type.145
  1.3 12.8 %all-gather = bf16[4,1,128]{2,1,0:T(2,128)(2,1)S(1)} all-gather(bf16[1,1,128]{2,1,0:T(2,128)(2,1)} %bitcast.188), channel_id=1, replica_groups=mesh['dp'=4,'blk'=2,'head'=4] {'dp'}, dimensions={0}, use_global_device_ids=true | all-gather | bytes 1280 | tf_op jit(solution)/shard_map/all_gather | solution.py:807
  14.1 0.6 copy-done.11
  14.7 0.9 convolution_add_fusion.2
  15.5 0.1 reshape.413
  15.6 2.8 concatenate.27
  18.4 0.6 pad_bitcast_fusion.1.refs_0_
  19.0 25.3 %gather.1 = (f32[32,8,128]{2,1,0:T(8,128)}, bf16[32,72,768]{2,1,0:T(8,128)(2,1)}) custom-call(f32[8,128]{1,0:T(8,128)} %pad_bitcast_fusion.1.refs_0_, bf16[72,768]{1,0:T(8,128)(2,1)} %bitcast.181), custom_call_target="tpu_custom_call" | custom-call | tf_op jit(solution)/shard_map/gather/pallas_call | solution.py:226
  44.3 0.9 copy.43
  45.3 0.1 reshape.416
  45.4 0.1 dynamic-slice_reduce_fusion
  46.4 0.1 mul.390
  46.5 1.1 convert_reduce_fusion.1
  47.7 1.2 fusion.23
  48.9 3.4 %fusion.58 = f32[2304,256]{1,0:T(8,128)S(1)} fusion(bf16[2304,768]{1,0:T(8,128)(2,1)} %bitcast.152, bf16[1,256,768]{2,1,0:T(8,128)(2,1)} %param.14, f32[768]{0:T(1024)S(1)} %get-tuple-element.64, f32[768]{0:T(1024)S(1)} %get-tuple-element.65, f32[768]{0:T(1024)S(1)} %mul.390, f32[256]{0:T(256)S(1)} %add_rsqrt_fusion.1, f32[256]{0:T(256)S(1)} %broadcast_multiply_fusion.5), kind=kOutput, calls=%fused_computation.132 | convolution fusion | flops 907345920 | bytes 6302720 | tf_op jit(solution)/shard_map/ed,td->et/dot_general | solution.py:779
  52.3 0.1 fusion.63
  52.5 0.2 fusion.49
  52.7 0.2 subtract_convert_fusion.3
  53.0 1.2 pad_maximum_fusion.qkv
  54.2 82.3 %attend.1 = (bf16[4,192,256]{2,1,0:T(8,128)(2,1)}, bf16[192,1024]{1,0:T(8,128)(2,1)}, bf16[192,2048]{1,0:T(8,128)(2,1)}, bf16[192,2048]{1,0:T(8,128)(2,1)}, f32[...) custom-call(s32[1]{0:T(128)} %copy.54.length_ref, ...), custom_call_target="tpu_custom_call" | custom-call | tf_op jit(solution)/shard_map/attend/pallas_call | solution.py:561
  136.5 2.0 fusion.61
  138.5 0.2 multiply_reduce_fusion.4
  139.0 3.9 %convolution_add_fusion = f32[256,3072]{1,0:T(8,128)S(1)} fusion(bf16[3072,768]{1,0:T(8,128)(2,1)} %bitcast.191, f32[3072]{0:T(1024)S(1)} %add.167, f32[256,768]{1,0:T(8,128)S(1)} %get-tuple-element.70, f32[768]{0:T(1024)S(1)} %get-tuple-element.62, f32[768]{0:T(1024)S(1)} %get-tuple-element.63, f32[768]{0:T(1024)S(1)} %mul.418, f32[256]{0:T(256)S(1)} %add_rsqrt_fusion, ...), kind=kOutput, calls=%fused_computation.5 | convolution fusion | flops 1209925632 | bytes 8674304 | tf_op jit(solution)/shard_map/td,fd->tf/dot_general | solution.py:779
  142.9 8.1 %convert_reduce_fusion = (f32[3072]{0:T(1024)}, bf16[256,3072]{1,0:T(8,128)(2,1)S(1)}) fusion(f32[256,3072]{1,0:T(8,128)S(1)} %convolution_add_fusion, bf16[768,3072]{1,0:T(8,128)(2,1)} %bitcast.189, bf16[1,256,768]{2,1,0:T(8,128)(2,1)S(1)} %copy-done.13, f32[768]{0:T(1024)S(1)} %get-tuple-element.61, f32[256]{0:T(256)S(1)} %compare_convert_fusion), kind=kOutput, calls=%fused_computation.13 | convolution fusion | flops 1226044416 | bytes 9846784 | tf_op jit(solution)/shard_map/td,df->tf/dot_general | solution.py:779
  151.0 3.1 multiply_reduce_fusion
  154.2 7.4 %convert_reduce_fusion.2 = (f32[768]{0:T(1024)}, f32[768]{0:T(1024)}, bf16[1,256,768]{2,1,0:T(8,128)(2,1)}, f32[768]{0:T(1024)}, f32[256,768]{1,0:T(8,128)S(1)}) fusion(f32[768]{0:T(1024)S(1)} %get-tuple-element.61, f32[256]{0:T(256)S(1)} %compare_convert_fusion, bf16[1,256,768]{2,1,0:T(8,128)(2,1)} %param.27, f32[256,768]{1,0:T(8,128)S(1)} %get-tuple-element.70, ...), kind=kOutput, calls=%fused_computation.59 | convolution fusion | flops 1219557120 | bytes 11823104 | tf_op jit(solution)/shard_map/tf,df->td/dot_general | solution.py:779
  161.5 1.3 convolution_convert_fusion.4
  162.8 1.6 convolution_convert_fusion.3
  164.4 3.7 %convolution_convert_fusion.2 = bf16[3072,768]{1,0:T(8,128)(2,1)} fusion(bf16[256,3072]{1,0:T(8,128)(2,1)S(1)} %copy-done.4, f32[256,768]{1,0:T(8,128)S(1)} %get-tuple-element.70, f32[768]{0:T(1024)S(1)} %get-tuple-element.62, f32[768]{0:T(1024)S(1)} %get-tuple-element.63, f32[768]{0:T(1024)S(1)} %mul.418, f32[256]{0:T(256)S(1)} %add_rsqrt_fusion, ...), kind=kOutput, calls=%fused_computation.2 | convolution fusion | flops 1211498496 | bytes 7089152 | tf_op jit(solution)/shard_map/tf,td->fd/dot_general | solution.py:779
  168.1 3.8 %convolution_convert_fusion.1 = bf16[768,3072]{1,0:T(8,128)(2,1)} fusion(bf16[1,256,768]{2,1,0:T(8,128)(2,1)S(1)} %copy-done.14, f32[256]{0:T(256)S(1)} %compare_convert_fusion, f32[768]{0:T(1024)S(1)} %get-tuple-element.61, f32[256,3072]{1,0:T(8,128)S(1)} %copy-done.16), kind=kOutput, calls=%fused_computation.1 | convolution fusion | flops 1218183168 | bytes 8261632 | tf_op jit(solution)/shard_map/td,tf->df/dot_general | solution.py:779
  171.9 81.4 %attend_back.1 = (bf16[3,4,192,256]{3,2,1,0:T(8,128)(2,1)}, f32[24,768]{1,0:T(8,128)}, f32[96,768]{1,0:T(8,128)}, f32[24,3072]{1,0:T(8,128)}) custom-call(s32[1]{0:T(128)} %copy.54.length_ref, bf16[4,192,256]{2,1,0:T(8,128)(2,1)} %bitcast.160, bf16[192,1024]{1,0:T(8,128)(2,1)} %get-tuple-element.37.qt, bf16[192,2048]{1,0:T(8,128)(2,1)} %get-tuple-element.38.kt, ...), custom_call_target="tpu_custom_call" | custom-call | tf_op jit(solution)/shard_map/attend_back/pallas_call | solution.py:714
  253.3 1.3 fusion.64
  254.8 0.2 subtract_convert_fusion.1
  255.1 0.1 pad_maximum_fusion.1
  255.3 1.5 copy-done.1
  256.8 1.9 fusion.22
  258.7 2.0 fusion.19
  260.7 0.7 constant_dynamic-update-slice_fusion.5
  261.4 0.7 constant_dynamic-update-slice_fusion.4
  262.1 0.7 constant_dynamic-update-slice_fusion.3
  262.8 0.7 constant_dynamic-update-slice_fusion.2
  263.5 0.7 constant_dynamic-update-slice_fusion.1
  264.1 0.7 constant_dynamic-update-slice_fusion
  265.0 0.1 broadcast_in_dim.96
  265.2 0.1 broadcast_in_dim.59
  265.3 0.8 reshape.427
  266.0 0.8 reshape.428
  266.8 0.8 reshape.429
  267.6 0.8 reshape.430
  268.4 0.6 convolution_bitcast_fusion.1
  269.2 0.1 concatenate.33
  269.3 0.7 copy.33
  270.0 3.7 %convolution_convert_fusion = bf16[2304,768]{1,0:T(8,128)(2,1)} fusion(bf16[2304,256]{1,0:T(8,128)(2,1)S(1)} %bitcast.151, bf16[1,256,768]{2,1,0:T(8,128)(2,1)S(1)} %copy-done, f32[768]{0:T(1024)S(1)} %get-tuple-element.64, f32[768]{0:T(1024)S(1)} %get-tuple-element.65, f32[768]{0:T(1024)S(1)} %mul.390, f32[256]{0:T(256)} %copy-done.10, ...), kind=kOutput, calls=%fused_computation | convolution fusion | flops 909115392 | bytes 5123072 | tf_op jit(solution)/shard_map/et,td->ed/dot_general | solution.py:779
  273.7 30.1 %reduce.16 = (f32[8,128]{1,0:T(8,128)}, f32[72,768]{1,0:T(8,128)}) custom-call(f32[32,8,128]{2,1,0:T(8,128)} %bitcast.173, bf16[32,72,768]{2,1,0:T(8,128)(2,1)} %bitcast.149), custom_call_target="tpu_custom_call" | custom-call | tf_op jit(solution)/shard_map/reduce/pallas_call | solution.py:257
  303.9 1.3 slice_bitcast_fusion
  305.1 0.8 reshape.436
  305.9 0.9 convolution_bitcast_fusion
  306.8 0.6 reduce_sum.189
  307.3 1.4 fusion.66
  308.7 1.3 slice.73
  310.0 1.6 copy.55
  311.6 0.6 copy.56
  312.3 0.7 copy.57
  313.0 0.7 copy.58
  (73 shorter events, 1.4 us)
Async XLA Ops:
  14.1 0.6 copy-start.11
  48.9 206.4 %copy-start.10 = (f32[256]{0:T(256)}, f32[256]{0:T(256)S(1)}, u32[]{:S(2)}) copy-start(f32[256]{0:T(256)S(1)} %add_rsqrt_fusion.1) | copy-start | bytes 3076
  52.9 83.5 %copy-start = (bf16[1,256,768]{2,1,0:T(8,128)(2,1)S(1)}, bf16[1,256,768]{2,1,0:T(8,128)(2,1)}, u32[]{:S(2)}) copy-start(bf16[1,256,768]{2,1,0:T(8,128)(2,1)} %param.14) | copy-start | bytes 1179652
  139.0 3.9 %copy-start.13 = (bf16[1,256,768]{2,1,0:T(8,128)(2,1)S(1)}, bf16[1,256,768]{2,1,0:T(8,128)(2,1)}, u32[]{:S(2)}) copy-start(bf16[1,256,768]{2,1,0:T(8,128)(2,1)} %param.27) | copy-start | bytes 1179652
  139.0 12.0 %slice-start = ((s8[4718592]{0:T(1024)(128)(4,1)}), s8[524288]{0:T(1024)(128)(4,1)S(1)}, s32[]{:S(2)}) async-start(s8[4718592]{0:T(1024)(128)(4,1)} %bitcast.192), calls=%async_computation | async-start | bytes 1048576
  142.9 8.1 %copy-start.15 = (f32[256,3072]{1,0:T(8,128)}, f32[256,3072]{1,0:T(8,128)S(1)}, u32[]{:S(2)}) copy-start(f32[256,3072]{1,0:T(8,128)S(1)} %convolution_add_fusion) | copy-start | bytes 9437188
  142.9 8.1 %slice-start.1 = ((s8[4718592]{0:T(1024)(128)(4,1)}), s8[4194304]{0:T(1024)(128)(4,1)S(1)}, s32[]{:S(2)}) async-start(s8[4718592]{0:T(1024)(128)(4,1)} %bitcast.192), calls=%async_computation.1 | async-start | bytes 8388608
  151.0 3.1 copy-start.3
  154.2 7.4 %copy-start.2 = (bf16[32,24,768]{2,1,0:T(8,128)(2,1)S(1)}, bf16[32,24,768]{2,1,0:T(8,128)(2,1)}, u32[]{:S(2)}) copy-start(bf16[32,24,768]{2,1,0:T(8,128)(2,1)} %get-tuple-element.34) | copy-start | bytes 3538948
  154.2 8.7 %copy-start.5 = (bf16[4,192,256]{2,1,0:T(8,128)(2,1)S(1)}, bf16[4,192,256]{2,1,0:T(8,128)(2,1)}, u32[]{:S(2)}) copy-start(bf16[4,192,256]{2,1,0:T(8,128)(2,1)} %get-tuple-element.33) | copy-start | bytes 1179652
  161.5 2.9 copy-start.4
  164.4 3.7 %copy-start.14 = (bf16[1,256,768]{2,1,0:T(8,128)(2,1)S(1)}, bf16[1,256,768]{2,1,0:T(8,128)(2,1)}, u32[]{:S(2)}) copy-start(bf16[1,256,768]{2,1,0:T(8,128)(2,1)} %param.27) | copy-start | bytes 1179652
  164.4 3.7 %copy-start.16 = (f32[256,3072]{1,0:T(8,128)S(1)}, f32[256,3072]{1,0:T(8,128)}, u32[]{:S(2)}) copy-start(f32[256,3072]{1,0:T(8,128)} %copy-done.15) | copy-start | bytes 9437188
  254.8 2.0 copy-start.1
  258.7 9.7 %copy-start.6 = (bf16[32,144,128]{2,1,0:T(8,128)(2,1)S(1)}, bf16[32,144,128]{2,1,0:T(8,128)(2,1)}, u32[]{:S(2)}) copy-start(bf16[32,144,128]{2,1,0:T(8,128)(2,1)} %get-tuple-element.43) | copy-start | bytes 3538948
  273.7 32.2 %copy-start.12 = (bf16[4,1,128]{2,1,0:T(2,128)(2,1)S(1)}, bf16[4,1,128]{2,1,0:T(2,128)(2,1)}, u32[]{:S(2)}) copy-start(bf16[4,1,128]{2,1,0:T(2,128)(2,1)} %copy-done.11) | copy-start | bytes 3076
  273.7 37.9 %copy-start.9 = (f32[24,768]{1,0:T(8,128)S(1)}, f32[24,768]{1,0:T(8,128)}, u32[]{:S(2)}) copy-start(f32[24,768]{1,0:T(8,128)} %get-tuple-element.46) | copy-start | bytes 221188
  273.7 38.5 %copy-start.8 = (f32[96,768]{1,0:T(8,128)S(1)}, f32[96,768]{1,0:T(8,128)}, u32[]{:S(2)}) copy-start(f32[96,768]{1,0:T(8,128)} %get-tuple-element.47) | copy-start | bytes 884740
  273.7 39.3 %copy-start.7 = (f32[24,3072]{1,0:T(8,128)S(1)}, f32[24,3072]{1,0:T(8,128)}, u32[]{:S(2)}) copy-start(f32[24,3072]{1,0:T(8,128)} %get-tuple-element.48) | copy-start | bytes 884740

commit v3 on v2

--- a/solution.py
+++ b/solution.py
@@ -804,26 +804,22 @@
     rows_all = topo.nd
     _, tok_count, width = tokens.shape
     slots = tok_count * topo.row
-    cond_all = lax.all_gather(cond, "dp", axis=0, tiled=True)
+    vectors = [norm1_gain, norm2_gain, up_bias, down_bias]
     mod_columns = ada_weight.shape[1]
-    mod_own = jnp.dot(cond_all, ada_weight, preferred_element_type=F32) + ada_bias.astype(F32)
-    vectors = [norm1_gain, norm2_gain, up_bias, down_bias]
-    small = jnp.concatenate([mod_own.reshape(-1)] + [v.astype(F32) for v in vectors])
+    small = jnp.concatenate([v.astype(F32) for v in (cond[0], ada_bias, *vectors)])
     small = jnp.pad(small, (0, -small.shape[0] % 1024)).reshape(-1, 128)
-    small_all, qkv_t = gather(topo, [small, qkv_weight.T], 0)
-    qkv_t = joined(qkv_t)
+    small_all, ada_t, qkv_t = gather(topo, [small, ada_weight.T, qkv_weight.T], 0)
+    ada_t, qkv_t = joined(ada_t), joined(qkv_t)
     small_all = small_all.reshape(devices, -1)
-    mod_all = small_all[:, : rows_all * mod_columns].reshape(devices, rows_all, mod_columns)
-    modulation = lax.dynamic_index_in_dim(
-        mod_all, lax.axis_index("dp"), 1, keepdims=False
-    ).reshape(6, 1, width)
-    shift_one, scale_one, gate_one, shift_two, scale_two, gate_two = modulation
-    cut = rows_all * mod_columns
+    cond_all = small_all[:: topo.row, : cond.shape[1]]
+    cut = cond.shape[1]
     full_vectors = []
-    for v in vectors:
+    for v in (ada_bias, *vectors):
         full_vectors.append(small_all[:, cut : cut + v.shape[0]].reshape(-1))
         cut += v.shape[0]
-    gain_one, gain_two, up_bias_full, down_bias_full = full_vectors
+    ada_bias_full, gain_one, gain_two, up_bias_full, down_bias_full = full_vectors
+    modulation = (product("rc,ec->re", cond, ada_t) + ada_bias_full).reshape(6, 1, width)
+    shift_one, scale_one, gate_one, shift_two, scale_two, gate_two = modulation
     seq_index = lax.axis_index("blk") * topo.nh + lax.axis_index("head")
     positions = seq_index * tok_count + jnp.arange(tok_count, dtype=jnp.int32)
     slot_live = (positions < lengths[0]).astype(F32)[:, None]
@@ -842,11 +838,11 @@
         topo,
         lengths,
         turned.reshape(3, topo.groups, -1, tok_count),
-        [out_weight.T, up_weight.T, down_weight.T, ada_weight.T],
+        [out_weight.T, up_weight.T, down_weight.T],
         slots,
         1,
     )
-    out_t, up_t, down_t, ada_t = (joined(w) for w in weights)
+    out_t, up_t, down_t = (joined(w) for w in weights)
     attended = joined(attended)
     branch_one = product("dt,ed->te", attended, out_t)
     middle = tokens_wide + gate_one * branch_one
@@ -946,7 +942,7 @@
         vector_grads.append(small_own[cut : cut + v.shape[0]])
         cut += v.shape[0]
     grad_cond = small_own[cut : cut + cond.shape[1]].reshape(1, -1)
-    grad_ada = jnp.dot(cond_all.astype(F32).T, mod_grads, precision=HIGHEST)
+    grad_ada = jnp.dot(cond_all.T, mod_grads, precision=HIGHEST)
     return (
         result.astype(BF16)[None],
         grad_tokens[None],

time: 318 us -> 310 us (0.975)
  blocking collectives: 12.8 us -> 0 us
  local copies, waits for them, and re-layouts: 25.7 us -> 32.9 us
  matrix products: 46.1 us -> 40.5 us
    all_gather x1 -> x0, blocking collectives: 12.8 us -> none  [body(): cond_all = lax.all_gather(cond, 'dp', axis=0, tiled=True)]
    pallas_call x1, Pallas kernels: 25.3 us -> 35.8 us  [gather(): pl.pallas_call(partial(gather_kernel, topo, count), out_shape=gathered_sh...]
    pallas_call x1, Pallas kernels: 82.3 us -> 76.8 us  [attend(): pl.pallas_call(partial(attend_kernel, topo, count), out_shape=shapes + ga...]
    dot_general x12 -> x13, matrix products: 43.8 us -> 39 us  [product(): return jnp.einsum(equation, left, right, preferred_element_type=F32)]
    unnamed x50 -> x58, local copies, waits for them, and re-layouts: 10.9 us -> 13.4 us
where the time goes in v3:
time: 310 us; the launch traced here: 306 us
  Pallas kernels  222 us (72%)
  matrix products  40.5 us (13%)
  local copies, waits for them, and re-layouts  32.9 us (11%)
  other arithmetic  8.75 us (3%)
    pallas_call x1, Pallas kernels, attend_back(): pl.pallas_call(partial(attend_back_kernel, topo, count), out_shape=[jax.S...  78.2 us
    pallas_call x1, Pallas kernels, attend(): pl.pallas_call(partial(attend_kernel, topo, count), out_shape=shapes + ga...  76.8 us
    dot_general x13, matrix products, product(): return jnp.einsum(equation, left, right, preferred_element_type=F32)  39 us
    pallas_call x1, Pallas kernels, gather(): pl.pallas_call(partial(gather_kernel, topo, count), out_shape=gathered_sh...  35.8 us
    pallas_call x1, Pallas kernels, reduce_scatter(): pl.pallas_call(partial(reduce_kernel, topo, count), out_shape=owned_shape...  31 us
    unnamed x58, local copies, waits for them, and re-layouts  13.4 us

profile of v3, /device:TPU:0, one launch (start us, length us, event | category | flops | bytes accessed | tf_op | source)
XLA Modules:
  0.0 306.0 jit_solution(14892370046658817334)
XLA Ops:
  1.4 0.6 broadcast_in_dim.98
  2.1 0.7 broadcast_in_dim.59
  2.8 4.1 %concatenate.28 = bf16[440]{0:T(512)(128)(2,1)S(1)} concatenate(bf16[128]{0:T(256)(128)(2,1)} %bitcast.188, bf16[144]{0:T(256)(128)(2,1)} %param.18, bf16[24]{0:T(256)(128)(2,1)} %param.19, bf16[24]{0:T(256)(128)(2,1)} %param.22, bf16[96]{0:T(256)(128)(2,1)} %param.24, bf16[24]{0:T(256)(128)(2,1)} %param.26), dimensions={0} | concatenate | bytes 1760 | tf_op jit(solution)/shard_map/concatenate | solution.py:809
  6.9 1.1 convert_reduce_fusion.1
  8.0 1.2 fusion.23
  9.3 0.6 bitcast_convert_fusion.refs_0_
  9.9 0.2 fusion.49
  10.1 35.8 %gather.1 = (f32[32,8,128]{2,1,0:T(8,128)}, bf16[32,144,128]{2,1,0:T(8,128)(2,1)}, bf16[32,72,768]{2,1,0:T(8,128)(2,1)}) custom-call(f32[8,128]{1,0:T(8,128)} %bitcast_convert_fusion.refs_0_, bf16[144,128]{1,0:T(8,128)(2,1)} %bitcast.183, bf16[72,768]{1,0:T(8,128)(2,1)} %bitcast.180), custom_call_target="tpu_custom_call" | custom-call | tf_op jit(solution)/shard_map/gather/pallas_call | solution.py:226
  45.8 0.9 copy.30
  46.8 0.6 slice.79
  47.5 1.7 convolution_reduce_fusion
  49.3 0.1 broadcast_in_dim_reshape.2
  49.7 3.4 %fusion.55 = f32[2304,256]{1,0:T(8,128)S(1)} fusion(bf16[2304,768]{1,0:T(8,128)(2,1)} %bitcast.150, bf16[1,256,768]{2,1,0:T(8,128)(2,1)} %param.14, f32[768]{0:T(1024)S(1)} %get-tuple-element.64, f32[768]{0:T(1024)S(1)} %get-tuple-element.65, f32[768]{0:T(1024)S(1)} %mul.394, f32[256]{0:T(256)S(1)} %add_rsqrt_fusion.1, f32[256]{0:T(256)S(1)} %broadcast_multiply_fusion.5), kind=kOutput, calls=%fused_computation.127 | convolution fusion | flops 907345920 | bytes 6302720 | tf_op jit(solution)/shard_map/ed,td->et/dot_general | solution.py:779
  53.2 0.1 fusion.60
  53.3 0.2 subtract_convert_fusion.3
  53.6 1.2 pad_maximum_fusion.qkv
  54.8 76.8 %attend.1 = (bf16[4,192,256]{2,1,0:T(8,128)(2,1)}, bf16[192,1024]{1,0:T(8,128)(2,1)}, bf16[192,2048]{1,0:T(8,128)(2,1)}, bf16[192,2048]{1,0:T(8,128)(2,1)}, f32[...) custom-call(s32[1]{0:T(128)} %copy.41.length_ref, ...), custom_call_target="tpu_custom_call" | custom-call | tf_op jit(solution)/shard_map/attend/pallas_call | solution.py:561
  131.6 2.0 fusion.58
  133.7 0.2 multiply_reduce_fusion.4
  133.9 4.0 %convolution_add_fusion = f32[256,3072]{1,0:T(8,128)S(1)} fusion(bf16[3072,768]{1,0:T(8,128)(2,1)} %bitcast.193, f32[3072]{0:T(1024)S(1)} %add.146, f32[256,768]{1,0:T(8,128)S(1)} %get-tuple-element.70, f32[768]{0:T(1024)S(1)} %get-tuple-element.62, f32[768]{0:T(1024)S(1)} %get-tuple-element.63, f32[768]{0:T(1024)S(1)} %mul.423, f32[256]{0:T(256)S(1)} %add_rsqrt_fusion, ...), kind=kOutput, calls=%fused_computation.5 | convolution fusion | flops 1209925632 | bytes 8674304 | tf_op jit(solution)/shard_map/td,fd->tf/dot_general | solution.py:779
  138.0 4.1 %convert_reduce_fusion = (f32[3072]{0:T(1024)S(1)}, bf16[256,3072]{1,0:T(8,128)(2,1)S(1)}) fusion(f32[256,3072]{1,0:T(8,128)S(1)} %convolution_add_fusion, bf16[768,3072]{1,0:T(8,128)(2,1)S(1)} %bitcast.191, bf16[1,256,768]{2,1,0:T(8,128)(2,1)S(1)} %copy-done.17, f32[768]{0:T(1024)S(1)} %get-tuple-element.61, f32[256]{0:T(256)S(1)} %compare_convert_fusion), kind=kOutput, calls=%fused_computation.13 | convolution fusion | flops 1226044416 | bytes 9846784 | tf_op jit(solution)/shard_map/td,df->tf/dot_general | solution.py:779
  142.1 2.2 multiply_reduce_fusion
  144.3 3.7 %convert_reduce_fusion.2 = (f32[768]{0:T(1024)S(1)}, f32[768]{0:T(1024)}, bf16[1,256,768]{2,1,0:T(8,128)(2,1)}, f32[768]{0:T(1024)}, f32[256,768]{1,0:T(8,128)S(1)}) fusion(f32[768]{0:T(1024)S(1)} %get-tuple-element.61, f32[256]{0:T(256)S(1)} %compare_convert_fusion, bf16[1,256,768]{2,1,0:T(8,128)(2,1)S(1)} %copy-done.17, ...), kind=kOutput, calls=%fused_computation.58 | convolution fusion | flops 1219557120 | bytes 11823104 | tf_op jit(solution)/shard_map/tf,df->td/dot_general | solution.py:779
  148.0 1.3 convolution_convert_fusion.4
  149.3 0.7 reshape.418
  149.9 0.7 reshape.419
  150.6 0.7 reshape.417
  151.3 1.5 convolution_convert_fusion.3
  152.9 5.8 %convolution_convert_fusion.1 = bf16[768,3072]{1,0:T(8,128)(2,1)} fusion(bf16[1,256,768]{2,1,0:T(8,128)(2,1)S(1)} %copy-done.17, f32[256]{0:T(256)S(1)} %compare_convert_fusion, f32[768]{0:T(1024)S(1)} %get-tuple-element.61, f32[256,3072]{1,0:T(8,128)} %copy-done.18), kind=kOutput, calls=%fused_computation.1 | convolution fusion | flops 1218183168 | bytes 8261632 | tf_op jit(solution)/shard_map/td,tf->df/dot_general | solution.py:779
  158.6 3.8 %convolution_convert_fusion.2 = bf16[3072,768]{1,0:T(8,128)(2,1)} fusion(bf16[256,3072]{1,0:T(8,128)(2,1)S(1)} %copy-done.5, f32[256,768]{1,0:T(8,128)S(1)} %get-tuple-element.70, f32[768]{0:T(1024)S(1)} %get-tuple-element.62, f32[768]{0:T(1024)S(1)} %get-tuple-element.63, f32[768]{0:T(1024)S(1)} %mul.423, f32[256]{0:T(256)S(1)} %add_rsqrt_fusion, ...), kind=kOutput, calls=%fused_computation.2 | convolution fusion | flops 1211498496 | bytes 7089152 | tf_op jit(solution)/shard_map/tf,td->fd/dot_general | solution.py:779
  162.4 78.2 %attend_back.1 = (bf16[3,4,192,256]{3,2,1,0:T(8,128)(2,1)}, f32[24,768]{1,0:T(8,128)}, f32[96,768]{1,0:T(8,128)}, f32[24,3072]{1,0:T(8,128)}) custom-call(s32[1]{0:T(128)} %copy.41.length_ref, bf16[4,192,256]{2,1,0:T(8,128)(2,1)} %bitcast.160, bf16[192,1024]{1,0:T(8,128)(2,1)} %get-tuple-element.38.qt, bf16[192,2048]{1,0:T(8,128)(2,1)} %get-tuple-element.39.kt, ...), custom_call_target="tpu_custom_call" | custom-call | tf_op jit(solution)/shard_map/attend_back/pallas_call | solution.py:714
  240.7 1.3 fusion.61
  242.1 0.2 subtract_convert_fusion.1
  242.5 0.1 pad_maximum_fusion.1
  242.6 1.5 copy-done.1
  244.2 1.9 fusion.22
  246.1 1.3 constant_dynamic-update-slice_fusion.5
  247.4 1.3 constant_dynamic-update-slice_fusion.4
  248.7 1.3 constant_dynamic-update-slice_fusion.3
  250.0 1.3 constant_dynamic-update-slice_fusion.2
  251.3 1.3 constant_dynamic-update-slice_fusion.1
  252.6 1.3 constant_dynamic-update-slice_fusion
  253.9 1.2 fusion.19
  255.1 0.8 reshape.416
  255.9 0.7 reshape.432
  256.6 0.6 convolution_bitcast_fusion
  257.2 0.8 broadcast_in_dim.93
  258.0 0.7 broadcast_select_fusion.1
  258.8 0.1 broadcast_in_dim.95
  258.9 0.7 broadcast_select_fusion
  259.6 0.8 concatenate.34
  260.5 0.7 copy.28
  261.2 3.7 %convolution_convert_fusion = bf16[2304,768]{1,0:T(8,128)(2,1)} fusion(bf16[2304,256]{1,0:T(8,128)(2,1)S(1)} %bitcast.149, bf16[1,256,768]{2,1,0:T(8,128)(2,1)S(1)} %copy-done, f32[768]{0:T(1024)S(1)} %get-tuple-element.64, f32[768]{0:T(1024)S(1)} %get-tuple-element.65, f32[768]{0:T(1024)S(1)} %mul.394, f32[256]{0:T(256)} %copy-done.10, ...), kind=kOutput, calls=%fused_computation | convolution fusion | flops 909115392 | bytes 5123072 | tf_op jit(solution)/shard_map/et,td->ed/dot_general | solution.py:779
  264.9 31.0 %reduce.16 = (f32[8,128]{1,0:T(8,128)}, f32[72,768]{1,0:T(8,128)}) custom-call(f32[32,8,128]{2,1,0:T(8,128)} %bitcast.169, bf16[32,72,768]{2,1,0:T(8,128)(2,1)} %bitcast.147), custom_call_target="tpu_custom_call" | custom-call | tf_op jit(solution)/shard_map/reduce/pallas_call | solution.py:257
  295.9 1.3 slice.83
  297.1 1.3 slice_bitcast_fusion
  298.4 1.4 fusion.63
  299.8 0.8 reshape.424
  300.5 0.6 reduce_sum.189
  301.1 1.0 fusion.64
  302.1 1.6 copy.42
  303.7 0.6 copy.43
  304.4 0.7 copy.44
  305.1 0.7 copy.45
  (80 shorter events, 1.2 us)
Async XLA Ops:
  9.2 45.5 %copy-start.10 = (f32[256]{0:T(256)}, f32[256]{0:T(256)S(1)}, u32[]{:S(2)}) copy-start(f32[256]{0:T(256)S(1)} %add_rsqrt_fusion.1) | copy-start | bytes 3076
  53.5 78.1 %copy-start = (bf16[1,256,768]{2,1,0:T(8,128)(2,1)S(1)}, bf16[1,256,768]{2,1,0:T(8,128)(2,1)}, u32[]{:S(2)}) copy-start(bf16[1,256,768]{2,1,0:T(8,128)(2,1)} %param.14) | copy-start | bytes 1179652
  133.7 4.2 %slice-start = ((s8[4718592]{0:T(1024)(128)(4,1)}), s8[4194304]{0:T(1024)(128)(4,1)S(1)}, s32[]{:S(2)}) async-start(s8[4718592]{0:T(1024)(128)(4,1)} %bitcast.189), calls=%async_computation | async-start | bytes 8388608
  133.9 4.0 %slice-start.1 = ((s8[4718592]{0:T(1024)(128)(4,1)}), s8[524288]{0:T(1024)(128)(4,1)S(1)}, s32[]{:S(2)}) async-start(s8[4718592]{0:T(1024)(128)(4,1)} %bitcast.189), calls=%async_computation.1 | async-start | bytes 1048576
  133.9 4.0 %copy-start.17 = (bf16[1,256,768]{2,1,0:T(8,128)(2,1)S(1)}, bf16[1,256,768]{2,1,0:T(8,128)(2,1)}, u32[]{:S(2)}) copy-start(bf16[1,256,768]{2,1,0:T(8,128)(2,1)} %param.27) | copy-start | bytes 1179652
  133.9 8.1 %slice-start.2 = ((s8[4718592]{0:T(1024)(128)(4,1)}), s8[524288]{0:T(1024)(128)(4,1)S(1)}, s32[]{:S(2)}) async-start(s8[4718592]{0:T(1024)(128)(4,1)} %bitcast.194), calls=%async_computation.2 | async-start | bytes 1048576
  137.9 6.3 %copy-start.18 = (f32[256,3072]{1,0:T(8,128)}, f32[256,3072]{1,0:T(8,128)S(1)}, u32[]{:S(2)}) copy-start(f32[256,3072]{1,0:T(8,128)S(1)} %convolution_add_fusion) | copy-start | bytes 9437188
  137.9 4.1 %slice-start.3 = ((s8[4718592]{0:T(1024)(128)(4,1)}), s8[4194304]{0:T(1024)(128)(4,1)S(1)}, s32[]{:S(2)}) async-start(s8[4718592]{0:T(1024)(128)(4,1)} %bitcast.194), calls=%async_computation.3 | async-start | bytes 8388608
  142.0 2.2 copy-start.4
  144.3 3.7 %copy-start.2 = (bf16[32,24,768]{2,1,0:T(8,128)(2,1)S(1)}, bf16[32,24,768]{2,1,0:T(8,128)(2,1)}, u32[]{:S(2)}) copy-start(bf16[32,24,768]{2,1,0:T(8,128)(2,1)} %get-tuple-element.35) | copy-start | bytes 3538948
  144.3 7.1 %copy-start.6 = (bf16[4,192,256]{2,1,0:T(8,128)(2,1)S(1)}, bf16[4,192,256]{2,1,0:T(8,128)(2,1)}, u32[]{:S(2)}) copy-start(bf16[4,192,256]{2,1,0:T(8,128)(2,1)} %get-tuple-element.34) | copy-start | bytes 1179652
  152.9 5.8 %copy-start.5 = (bf16[256,3072]{1,0:T(8,128)(2,1)S(1)}, bf16[256,3072]{1,0:T(8,128)(2,1)}, u32[]{:S(2)}) copy-start(bf16[256,3072]{1,0:T(8,128)(2,1)} %copy-done.4) | copy-start | bytes 4718596
  242.1 2.0 copy-start.1
  242.1 2.0 copy-start.11
  244.1 4.6 %copy-start.16 = (f32[768]{0:T(1024)S(1)}, f32[768]{0:T(1024)}, u32[]{:S(2)}) copy-start(f32[768]{0:T(1024)} %get-tuple-element.85) | copy-start | bytes 9220
  244.1 5.9 %copy-start.14 = (f32[768]{0:T(1024)S(1)}, f32[768]{0:T(1024)}, u32[]{:S(2)}) copy-start(f32[768]{0:T(1024)} %get-tuple-element.57) | copy-start | bytes 9220
  244.1 7.2 %copy-start.13 = (f32[768]{0:T(1024)S(1)}, f32[768]{0:T(1024)}, u32[]{:S(2)}) copy-start(f32[768]{0:T(1024)} %get-tuple-element.51) | copy-start | bytes 9220
  244.1 8.5 %copy-start.15 = (f32[768]{0:T(1024)S(1)}, f32[768]{0:T(1024)}, u32[]{:S(2)}) copy-start(f32[768]{0:T(1024)} %get-tuple-element.60) | copy-start | bytes 9220
  244.1 12.5 %copy-start.3 = (bf16[32,144,128]{2,1,0:T(8,128)(2,1)S(1)}, bf16[32,144,128]{2,1,0:T(8,128)(2,1)}, u32[]{:S(2)}) copy-start(bf16[32,144,128]{2,1,0:T(8,128)(2,1)} %get-tuple-element.31) | copy-start | bytes 3538948
  264.8 36.3 %copy-start.12 = (f32[4,128]{1,0:T(4,128)S(1)}, f32[4,128]{1,0:T(4,128)}, u32[]{:S(2)}) copy-start(f32[4,128]{1,0:T(4,128)} %slice.79) | copy-start | bytes 6148
  264.8 38.9 %copy-start.9 = (f32[24,768]{1,0:T(8,128)S(1)}, f32[24,768]{1,0:T(8,128)}, u32[]{:S(2)}) copy-start(f32[24,768]{1,0:T(8,128)} %get-tuple-element.46) | copy-start | bytes 221188
  264.9 39.5 %copy-start.8 = (f32[96,768]{1,0:T(8,128)S(1)}, f32[96,768]{1,0:T(8,128)}, u32[]{:S(2)}) copy-start(f32[96,768]{1,0:T(8,128)} %get-tuple-element.47) | copy-start | bytes 884740
  264.9 40.2 %copy-start.7 = (f32[24,3072]{1,0:T(8,128)S(1)}, f32[24,3072]{1,0:T(8,128)}, u32[]{:S(2)}) copy-start(f32[24,3072]{1,0:T(8,128)} %get-tuple-element.48) | copy-start | bytes 884740
